TPU v7x, 512 devices: a whole 4x8x8 slice. The times are simulated.
512 devices in a mesh: fsdp: 16 (over z, core), req: 32 (over y, x).
Axes of the slice: x: 4, y: 8, z: 8, core: 2. Of those that a mesh axis runs over, the one named last changes fastest.
Arguments:
- drafts: bfloat16 [32, 16, 2560], P('req'), may hold values from -6 to 6
- x_weight: bfloat16 [2560, 5120], P('req', 'fsdp'), may hold values from -0.125 to 0.125
- z_weight: bfloat16 [2560, 5120], P('req', 'fsdp'), may hold values from -0.125 to 0.125
- bc_weight: bfloat16 [2560, 256], P('req'), may hold values from -0.125 to 0.125
- dt_weight: bfloat16 [2560, 80], P('req', 'fsdp'), may hold values from -0.125 to 0.125
- dt_bias: float32 [80], P('fsdp'), may hold values from -3 to 0
- decay_rate: float32 [80], P('fsdp'), may hold values from 0.01 to 0.5
- conv_x_weight: bfloat16 [4, 5120], P(None, 'fsdp'), may hold values from -3 to 3
- conv_x_bias: bfloat16 [5120], P('fsdp'), may hold values from -2 to 2
- conv_bc_weight: bfloat16 [4, 256], replicated, may hold values from -3 to 3
- conv_bc_bias: bfloat16 [256], replicated, may hold values from -2 to 2
- norm_gain: bfloat16 [5120], P('fsdp'), may hold values from 0.5 to 1.5
- out_weight: bfloat16 [5120, 2560], P('fsdp', 'req'), may hold values from -0.078125 to 0.078125
- conv_x_state: bfloat16 [32, 3, 5120], P('req', None, 'fsdp'), may hold values from -6 to 6
- conv_bc_state: bfloat16 [32, 3, 256], P('req'), may hold values from -6 to 6
- ssm_state: float32 [32, 80, 64, 128], P('req', 'fsdp'), may hold values from -6 to 6
- sink_x: bfloat16 [32, 4, 5120], P('req', None, 'fsdp'), may hold values from -12 to 12
- sink_b: bfloat16 [32, 4, 128], P('req'), may hold values from -6 to 6
- page_x: bfloat16 [320, 256, 5120], P('req', None, 'fsdp'), may hold values from -3 to 3
- page_b: bfloat16 [320, 256, 128], P('req'), may hold values from -6 to 6
- page_decay: float32 [320, 80, 256], P('req', 'fsdp')
- slot_req: int32 [320], P('req'), may hold values from -1 to 31, as said below
- slot_page: int32 [320], P('req'), may hold values from 0 to 15, as said below
- page_count: int32 [32], replicated, may hold values from 1 to 16, as said below
- accepted: int32 [32], P('req'), may hold values from 1 to 16
- owner_row: int32 [32], replicated, may hold values from 0 to 31, each once
Outputs:
- mixed: bfloat16 [32, 16, 2560], P('req', None, 'fsdp')
- new_state: float32 [32, 80, 64, 128], P('req', 'fsdp')
- new_conv_x: bfloat16 [32, 3, 5120], P('req', None, 'fsdp')
- new_conv_bc: bfloat16 [32, 3, 256], P('req')
Inputs may be any that keep to these rules, and one draw needn't show every extreme that they name: `page_count`: one request has 16 pages. `slot_req`: -1 marks an empty slot. Each page 0 to page_count - 1 of every request stands in exactly one slot; a request with fewer than 16 pages also has its page numbered page_count in one slot. `slot_page`: 0 in empty slots. `owner_row`: each row once.
All inputs are finite; a program needn't handle non-finite values.
Results may differ from a plain program's by a relative error of at most 0.015.
Values may be sent and summed in bfloat16 or wider, within the bound.
A program may use at most 64 MiB of HBM per device.

v0:
```python
import jax
import jax.numpy as jnp
from jax import lax
from jax.sharding import PartitionSpec as P

HD = 64
NS = 128
KC = 4
E = 5120


EPSILON = 1e-05


def conv_silu(history, fresh, kernel, offset):
    joined = jnp.concatenate([history, fresh], axis=1).astype(jnp.float32)
    length = fresh.shape[1]
    summed = offset.astype(jnp.float32) + jnp.zeros(fresh.shape, jnp.float32)
    for kernel_tap in range(KC):
        summed = (
            summed
            + kernel[kernel_tap].astype(jnp.float32) * joined[:, kernel_tap : kernel_tap + length]
        )
    return jax.nn.silu(summed).astype(jnp.bfloat16)


def local_terms(c_mat, b_mat, x_act, dtime, cumul, sink_x, sink_b):
    requests, length, head_count = dtime.shape
    inner = jnp.einsum("rtn,run->rtu", c_mat, b_mat, preferred_element_type=jnp.float32)
    later = jnp.arange(length)[:, None] >= jnp.arange(length)[None, :]
    spread = jnp.where(later[None, :, :, None], cumul[:, :, None, :] - cumul[:, None, :, :], 0.0)
    draft_weight = jnp.where(
        later[None, :, :, None], inner[..., None] * jnp.exp(spread) * dtime[:, None, :, :], 0.0
    ).astype(jnp.bfloat16)
    head_values = x_act.reshape(requests, length, head_count, HD)
    own_terms = jnp.einsum(
        "rtuh,ruhp->rthp", draft_weight, head_values, preferred_element_type=jnp.float32
    )
    sink_weight = jnp.einsum(
        "rtn,rsn->rts", c_mat, sink_b, preferred_element_type=jnp.float32
    ).astype(jnp.bfloat16)
    sink_terms = jnp.einsum("rts,rse->rte", sink_weight, sink_x, preferred_element_type=jnp.float32)
    return own_terms.reshape(requests, length, head_count * HD) + sink_terms


def page_batch(c_all, cumul_all, page_x, page_b, page_decay, slot_rows, slot_live, req_total):
    slot_count, page_len, inner_local = page_x.shape
    head_count = page_decay.shape[1]
    length = c_all.shape[1]
    queries = c_all[slot_rows]
    decay_q = cumul_all[slot_rows]
    scores = jnp.einsum("stn,spn->stp", queries, page_b, preferred_element_type=jnp.float32)
    weights = (
        scores[:, None]
        * jnp.exp(jnp.transpose(decay_q, (0, 2, 1))[:, :, :, None] - page_decay[:, :, None, :])
    ).astype(jnp.bfloat16)
    values = page_x.reshape(slot_count, page_len, head_count, HD)
    terms = jnp.einsum(
        "shtp,sphd->sthd", weights, values, preferred_element_type=jnp.float32
    ).reshape(slot_count, length * inner_local)
    selector = ((slot_rows[:, None] == jnp.arange(req_total)[None, :]) & slot_live[:, None]).astype(
        jnp.float32
    )
    summed = jnp.dot(selector.T, terms, precision=lax.Precision.HIGHEST)
    return summed.reshape(req_total, length, inner_local)


def per_device(
    drafts,
    x_weight,
    z_weight,
    bc_weight,
    dt_weight,
    dt_bias,
    decay_rate,
    conv_x_weight,
    conv_x_bias,
    conv_bc_weight,
    conv_bc_bias,
    norm_gain,
    out_weight,
    conv_x_state,
    conv_bc_state,
    ssm_state,
    sink_x,
    sink_b,
    page_x,
    page_b,
    page_decay,
    slot_req,
    slot_page,
    page_count,
    accepted,
    owner_row,
):
    req_total = owner_row.shape[0]
    local_reqs, length, width = drafts.shape
    token_rows = local_reqs * length
    inner_local = x_weight.shape[1]
    head_count = dt_weight.shape[1]
    flat_tokens = drafts.reshape(token_rows, width)
    pieces = (
        lax.all_gather(x_weight, "req", axis=0, tiled=True),
        lax.all_gather(z_weight, "req", axis=0, tiled=True),
        lax.all_gather(bc_weight, "req", axis=0, tiled=True),
        lax.all_gather(dt_weight, "req", axis=0, tiled=True),
    )
    x_proj, z_proj, bc_proj, dt_proj = tuple(
        (
            jnp.dot(flat_tokens, weight_rows, preferred_element_type=jnp.float32)
            for weight_rows in pieces
        )
    )
    x_raw = x_proj.astype(jnp.bfloat16).reshape(local_reqs, length, inner_local)
    z_raw = z_proj.astype(jnp.bfloat16).reshape(local_reqs, length, inner_local)
    bc_raw = bc_proj.astype(jnp.bfloat16).reshape(local_reqs, length, 2 * NS)
    dt_raw = dt_proj.reshape(local_reqs, length, head_count)
    x_act = conv_silu(conv_x_state, x_raw, conv_x_weight, conv_x_bias)
    bc_act = conv_silu(conv_bc_state, bc_raw, conv_bc_weight, conv_bc_bias)
    b_mat = bc_act[:, :, :NS]
    c_mat = bc_act[:, :, NS:]
    dtime = jax.nn.softplus(dt_raw + dt_bias)
    cumul = jnp.cumsum(-decay_rate * dtime, axis=1)
    c_wide, cumul_all = (
        lax.all_gather(c_mat.astype(jnp.float32), "req", axis=0, tiled=True),
        lax.all_gather(cumul, "req", axis=0, tiled=True),
    )
    c_all = c_wide.astype(jnp.bfloat16)
    guarded_query_index = jnp.maximum(slot_req, 0)
    slot_live = (slot_req >= 0) & (slot_page < page_count[guarded_query_index])
    slot_rows = owner_row[guarded_query_index]
    partial_value = page_batch(
        c_all, cumul_all, page_x, page_b, page_decay, slot_rows, slot_live, req_total
    )
    page_sum = lax.psum_scatter(partial_value, "req", scatter_dimension=0, tiled=True)
    head_values = x_act.astype(jnp.float32).reshape(local_reqs, length, head_count, HD)
    mixer_out = page_sum + local_terms(c_mat, b_mat, x_act, dtime, cumul, sink_x, sink_b)
    gated = mixer_out * jax.nn.silu(z_raw.astype(jnp.float32))
    square_sum = lax.psum(jnp.sum(gated * gated, axis=-1), "fsdp")
    normed = (
        gated * lax.rsqrt(square_sum / E + EPSILON)[..., None] * norm_gain.astype(jnp.float32)
    ).astype(jnp.bfloat16)
    normed_flat = normed.reshape(token_rows, inner_local)
    full_out = jnp.dot(
        normed_flat,
        lax.all_gather(out_weight, "req", axis=1, tiled=True),
        preferred_element_type=jnp.float32,
    )
    mixed = (
        lax.psum_scatter(full_out, "fsdp", scatter_dimension=1, tiled=True)
        .astype(jnp.bfloat16)
        .reshape(local_reqs, length, -1)
    )
    positions = jnp.arange(length)
    chosen = positions[None, :] == accepted[:, None] - 1
    cumul_last = jnp.sum(jnp.where(chosen[:, :, None], cumul, 0.0), axis=1)
    kept = positions[None, :] < accepted[:, None]
    state_spread = jnp.where(kept[:, :, None], cumul_last[:, None, :] - cumul, 0.0)
    coeff = jnp.where(kept[:, :, None], jnp.exp(state_spread) * dtime, 0.0)
    fresh_state = jnp.einsum(
        "ruh,ruhp,run->rhpn",
        coeff,
        head_values,
        b_mat.astype(jnp.float32),
        precision=lax.Precision.HIGHEST,
    )
    new_state = jnp.exp(cumul_last)[:, :, None, None] * ssm_state + fresh_state

    def tail_rows(history, fresh_rows):
        joined_rows = jnp.concatenate([history, fresh_rows], axis=1)
        return jax.vmap(
            lambda seq_rows, first_pos: lax.dynamic_slice_in_dim(seq_rows, first_pos, KC - 1, 0)
        )(joined_rows, accepted)

    new_conv_x = tail_rows(conv_x_state, x_raw)
    new_conv_bc = tail_rows(conv_bc_state, bc_raw)
    return (mixed, new_state, new_conv_x, new_conv_bc)


def solution(mesh):
    in_specs = (
        P("req", None, None),
        P("req", "fsdp"),
        P("req", "fsdp"),
        P("req", None),
        P("req", "fsdp"),
        P("fsdp"),
        P("fsdp"),
        P(None, "fsdp"),
        P("fsdp"),
        P(),
        P(),
        P("fsdp"),
        P("fsdp", "req"),
        P("req", None, "fsdp"),
        P("req", None, None),
        P("req", "fsdp", None, None),
        P("req", None, "fsdp"),
        P("req", None, None),
        P("req", None, "fsdp"),
        P("req", None, None),
        P("req", "fsdp", None),
        P("req"),
        P("req"),
        P(),
        P("req"),
        P(),
    )
    out_specs = (
        P("req", None, "fsdp"),
        P("req", "fsdp", None, None),
        P("req", None, "fsdp"),
        P("req", None, None),
    )
    return jax.shard_map(
        per_device, mesh=mesh, in_specs=in_specs, out_specs=out_specs, check_vma=False
    )
```

profile of v0, /device:TPU:1, one launch (start us, length us, event | category | flops | bytes accessed | tf_op | source)
XLA Modules:
  0.0 640.7 jit_solution(2369575452653982576)
XLA Ops:
  7.3 0.7 all-gather.6.cloned.1.call-update
  8.0 0.7 all-gather.8.cloned.1.call-update
  8.8 0.7 all-gather.10.cloned.1.call-update
  9.5 0.7 convert_element_type.158
  10.2 39.1 %all-gather = bf16[32,80,5]{1,2,0:T(8,128)(2,1)S(1)} all-gather(bf16[1,80,5]{1,2,0:T(8,128)(2,1)} %bitcast.115), channel_id=1, replica_groups=mesh['fsdp'=16,'req'=32] {'req'}, dimensions={0}, use_global_device_ids=true | all-gather | bytes 26400 | tf_op jit(solution)/shard_map/all_gather | solution.py:106
  49.2 0.1 reshape.468
  49.4 0.7 neg.21
  50.0 1.0 compare_select_fusion
  51.1 0.1 copy.47
  51.3 0.1 copy.48
  51.3 0.7 broadcast_maximum_fusion
  52.0 1.4 gather_fusion
  53.4 1.3 gather_fusion.1
  54.7 31.3 %all_gather.24 = f32[32,16,5]{1,2,0:T(8,128)S(1)} all-gather(f32[1,16,5]{1,2,0:T(8,128)S(1)} %copy.48), channel_id=1, replica_groups=mesh['fsdp'=16,'req'=32] {'req'}, dimensions={0}, use_global_device_ids=true | all-gather | bytes 10560 | tf_op jit(solution)/shard_map/all_gather | solution.py:126
  86.0 0.6 gather_fusion.3
  86.6 7.7 %all-gather.6.cloned.1.call-done = bf16[2560,256]{1,0:T(8,128)(2,1)} async-done(((bf16[80,256]{1,0:T(8,128)(2,1)}), bf16[2560,256]{1,0:T(8,128)(2,1)}) %all-gather.6.cloned.1.call-update) | async-done | bytes 1310736 | tf_op jit(solution)/shard_map/all_gather | solution.py:105
  94.4 1.6 fusion.6
  96.0 30.9 %all_gather.22 = bf16[32,16,128]{2,1,0:T(8,128)(2,1)S(1)} all-gather(bf16[1,16,128]{2,1,0:T(8,128)(2,1)S(1)} %slice.199), channel_id=1, replica_groups=mesh['fsdp'=16,'req'=32] {'req'}, dimensions={0}, use_global_device_ids=true | all-gather | bytes 135168 | tf_op jit(solution)/shard_map/all_gather | solution.py:125
  126.9 0.6 gather_fusion.2
  127.5 0.3 fusion.67
  127.8 0.6 convolution_bitcast_fusion.1
  128.4 0.2 copy.49
  128.6 0.2 reshape.367
  128.8 0.1 dot_general.59
  128.9 0.6 fusion.10
  129.5 1.4 copy.51
  130.9 0.5 all-gather.12.cloned.1.call-update
  132.2 0.1 select_reduce_fusion
  132.3 0.1 multiply_select_fusion
  132.4 0.1 copy.55
  132.5 0.6 fusion.58
  133.2 0.1 fusion.42
  133.3 45.8 %all-gather.8.cloned.1.call-done = bf16[2560,320]{1,0:T(8,128)(2,1)} async-done(((bf16[80,320]{1,0:T(8,128)(2,1)}), bf16[2560,320]{1,0:T(8,128)(2,1)}) %all-gather.8.cloned.1.call-update) | async-done | bytes 1638416 | tf_op jit(solution)/shard_map/all_gather | solution.py:103
  179.1 1.9 fusion.5
  181.1 0.1 reshape.368
  181.2 0.2 convolution_bitcast_fusion.3
  181.5 0.1 convert_multiply_fusion
  181.5 81.3 %all-gather.10.cloned.1.call-done = bf16[2560,320]{1,0:T(8,128)(2,1)} async-done(((bf16[80,320]{1,0:T(8,128)(2,1)}), bf16[2560,320]{1,0:T(8,128)(2,1)}) %all-gather.10.cloned.1.call-update) | async-done | bytes 1638416 | tf_op jit(solution)/shard_map/all_gather | solution.py:104
  262.9 1.9 fusion.4
  264.8 217.9 %reduce-scatter.5.cloned.1.call-done = f32[1,16,320]{2,1,0:T(8,128)} async-done(((f32[32,16,320]{2,1,0:T(8,128)}), f32[1,16,320]{2,1,0:T(8,128)}) %reduce-scatter.5.cloned.1.call-update) | async-done | bytes 20496 | tf_op jit(solution)/shard_map/reduce_scatter | solution.py:135
  482.7 1.2 multiply_reduce_fusion
  483.8 29.8 %psum.7 = f32[1,16]{1,0:T(1,128)S(1)} all-reduce(f32[1,16]{1,0:T(1,128)S(1)} %bitcast.116), channel_id=1, replica_groups=mesh['fsdp'=16,'req'=32] {'fsdp'}, use_global_device_ids=true, to_apply=%region_3.4 | all-reduce | flops 16 | bytes 128 | tf_op jit(solution)/shard_map/psum | solution.py:139
  513.7 55.0 %all-gather.12.cloned.1.call-done = bf16[320,2560]{0,1:T(8,128)(2,1)} async-done(((bf16[320,80]{0,1:T(8,128)(2,1)}), bf16[320,2560]{0,1:T(8,128)(2,1)}) %all-gather.12.cloned.1.call-update) | async-done | bytes 1638416 | tf_op jit(solution)/shard_map/all_gather | solution.py:146
  568.7 3.4 convolution_bitcast_fusion
  572.1 0.6 fusion.56
  572.7 1.0 fusion
  573.7 58.6 %reduce-scatter.7.cloned.1.call-done = f32[160,16]{1,0:T(8,128)} async-done(((f32[2560,16]{1,0:T(8,128)}), f32[160,16]{1,0:T(8,128)}) %reduce-scatter.7.cloned.1.call-update) | async-done | bytes 10256
  632.3 1.6 copy.58
  (61 shorter events, 0.8 us)
Async XLA Ops:
  7.2 120.6 %copy-start = (bf16[10,256,320]{1,2,0:T(8,128)(2,1)S(1)}, bf16[10,256,320]{1,2,0:T(8,128)(2,1)}, u32[]{:S(2)}) copy-start(bf16[10,256,320]{1,2,0:T(8,128)(2,1)} %param.44) | copy-start | bytes 4915204
  7.2 87.2 %copy-start.1 = (bf16[1,16,2560]{2,1,0:T(8,128)(2,1)S(1)}, bf16[1,16,2560]{2,1,0:T(8,128)(2,1)}, u32[]{:S(2)}) copy-start(bf16[1,16,2560]{2,1,0:T(8,128)(2,1)} %param.26) | copy-start | bytes 245764
  7.2 79.4 %copy-start.11 = (s32[10]{0:T(128)S(1)}, s32[10]{0:T(128)}, u32[]{:S(2)}) copy-start(s32[10]{0:T(128)} %param.47) | copy-start | bytes 124
  7.2 79.4 %copy-start.12 = (s32[10]{0:T(128)S(1)}, s32[10]{0:T(128)}, u32[]{:S(2)}) copy-start(s32[10]{0:T(128)} %param.48) | copy-start | bytes 124
  7.2 79.4 %copy-start.8 = (bf16[4,256]{1,0:T(4,128)(2,1)S(1)}, bf16[4,256]{1,0:T(4,128)(2,1)}, u32[]{:S(2)}) copy-start(bf16[4,256]{1,0:T(4,128)(2,1)} %param.35) | copy-start | bytes 6148
  7.2 88.7 %copy-start.7 = (bf16[1,3,256]{2,1,0:T(4,128)(2,1)S(1)}, bf16[1,3,256]{2,1,0:T(4,128)(2,1)}, u32[]{:S(2)}) copy-start(bf16[1,3,256]{2,1,0:T(4,128)(2,1)} %param.40) | copy-start | bytes 4612
  7.2 120.2 %copy-start.2 = (bf16[10,256,128]{2,1,0:T(8,128)(2,1)S(1)}, bf16[10,256,128]{2,1,0:T(8,128)(2,1)}, u32[]{:S(2)}) copy-start(bf16[10,256,128]{2,1,0:T(8,128)(2,1)} %param.45) | copy-start | bytes 1966084
  7.2 87.1 %all-gather.6.cloned.1.call-start = ((), (), s32[]{:S(2)}) async-start(), calls=%async_computation.2 | async-start | bytes 1351680 | tf_op jit(solution)/shard_map/all_gather | solution.py:105
  8.0 171.1 %all-gather.8.cloned.1.call-start = ((), (), s32[]{:S(2)}) async-start(), calls=%async_computation.4 | async-start | bytes 2027520 | tf_op jit(solution)/shard_map/all_gather | solution.py:103
  8.7 254.1 %all-gather.10.cloned.1.call-start = ((), (), s32[]{:S(2)}) async-start(), calls=%async_computation.5 | async-start | bytes 2027520 | tf_op jit(solution)/shard_map/all_gather | solution.py:104
  9.5 473.2 %reduce-scatter.5.cloned.1.call-start = ((), (), s32[]{:S(2)}) async-start(), calls=%async_computation.3 | async-start | bytes 811008 | tf_op jit(solution)/shard_map/reduce_scatter | solution.py:135
  52.0 75.8 %copy-start.4 = (f32[10,5,256]{2,1,0:T(8,128)S(1)}, f32[10,5,256]{2,1,0:T(8,128)}, u32[]{:S(2)}) copy-start(f32[10,5,256]{2,1,0:T(8,128)} %param.46) | copy-start | bytes 153604
  128.7 2.8 copy-start.9
  128.8 2.8 copy-start.10
  128.9 3.6 copy-start.5
  129.5 51.5 %copy-start.6 = (bf16[1,3,320]{2,1,0:T(4,128)(2,1)S(1)}, bf16[1,3,320]{2,1,0:T(4,128)(2,1)}, u32[]{:S(2)}) copy-start(bf16[1,3,320]{2,1,0:T(4,128)(2,1)} %param.39) | copy-start | bytes 5764
  130.9 437.8 %all-gather.12.cloned.1.call-start = ((), (), s32[]{:S(2)}) async-start(), calls=%async_computation.6 | async-start | bytes 2027520 | tf_op jit(solution)/shard_map/all_gather | solution.py:146
  131.5 500.8 %reduce-scatter.7.cloned.1.call-start = ((), (), s32[]{:S(2)}) async-start(), calls=%async_computation.7 | async-start | bytes 1392640
  133.3 349.4 %copy-start.13 = (bf16[1,4,320]{2,1,0:T(4,128)(2,1)S(1)}, bf16[1,4,320]{2,1,0:T(4,128)(2,1)}, u32[]{:S(2)}) copy-start(bf16[1,4,320]{2,1,0:T(4,128)(2,1)} %param.42) | copy-start | bytes 7684
  133.3 349.4 %copy-start.14 = (bf16[1,4,128]{2,1,0:T(4,128)(2,1)S(1)}, bf16[1,4,128]{2,1,0:T(4,128)(2,1)}, u32[]{:S(2)}) copy-start(bf16[1,4,128]{2,1,0:T(4,128)(2,1)} %param.43) | copy-start | bytes 3076
  568.7 4.0 copy-start.3
Sparse Core Ops, SparseCore 0:
  11.2 83.0 all-gather.5
  97.6 81.4 all-gather.7
  182.3 80.5 all-gather.9
  267.1 215.5 reduce-scatter.4
  485.7 82.9 all-gather.11
  572.2 60.0 reduce-scatter.6
where the time goes:
time: 643 us; the launch traced here: 641 us
  waiting for transfers between devices  469 us (73%)
  blocking collectives  131 us (20%)
  between operations  15.1 us (2%)
  matrix products  13.8 us (2%)
  local copies, waits for them, and re-layouts  7.82 us (1%)
    reduce_scatter x1, waiting for transfers between devices, per_device(): lax.psum_scatter(partial_value, 'req', scatter_dimension=0, tiled=True)  218 us
    all_gather x1, waiting for transfers between devices, per_device(): lax.all_gather(z_weight, 'req', axis=0, tiled=True)  81.3 us
    unnamed x7, waiting for transfers between devices  61.2 us
    all_gather x1, waiting for transfers between devices, per_device(): lax.all_gather(out_weight, 'req', axis=1, tiled=True)  55 us
    all_gather x1, waiting for transfers between devices, per_device(): lax.all_gather(x_weight, 'req', axis=0, tiled=True)  45.8 us
    all_gather x1, blocking collectives, per_device(): lax.all_gather(dt_weight, 'req', axis=0, tiled=True)  39.1 us
    all_gather x1, blocking collectives, per_device(): lax.all_gather(cumul, 'req', axis=0, tiled=True)  31.3 us
    all_gather x1, blocking collectives, per_device(): lax.all_gather(c_mat.astype(jnp.float32), 'req', axis=0, tiled=True)  30.9 us
  transfers between devices with their start and end apart: 6, of which 6 were waited for; matrix products, arithmetic and copies ran while one was open for 3% of the time, Pallas kernels for 0%

commit v1 on v0

v1 whole, which is shorter than its diff:
```python
import functools

import jax
import jax.numpy as jnp
from jax import lax
from jax.experimental import pallas as pl
from jax.experimental.pallas import tpu as pltpu
from jax.sharding import PartitionSpec as P

MESH = pl.DeviceIdType.MESH
T = 16
KC = 4
HD = 64
LN = 128
EPSILON = 1e-05
f32 = jnp.float32
bf16 = jnp.bfloat16
EXACT = lax.Precision.HIGHEST


def nt(a, b, precision=None):
    return lax.dot_general(
        a, b, (((1,), (1,)), ((), ())), preferred_element_type=f32, precision=precision
    )


def iota(shape, axis):
    return lax.broadcasted_iota(jnp.int32, shape, axis)


def silu(v):
    return v * jax.nn.sigmoid(v)


def pieces3(v):
    hi = v.astype(bf16).astype(f32)
    rest = v - hi
    mid = rest.astype(bf16).astype(f32)
    low = (rest - mid).astype(bf16).astype(f32)
    return hi, mid, low


def kernel(
    R,
    F,
    drafts_ref,
    xw_ref,
    zw_ref,
    bcw_ref,
    dtw_ref,
    dt_bias_ref,
    decay_ref,
    cxw_ref,
    cxb_ref,
    cbw_ref,
    cbb_ref,
    gain_ref,
    ow_ref,
    cxs_ref,
    cbs_ref,
    ssm_ref,
    sink_x_ref,
    sink_b_ref,
    page_x_ref,
    page_b_ref,
    page_decay_ref,
    slot_req_ref,
    slot_page_ref,
    page_count_ref,
    accepted_ref,
    owner_row_ref,
    mixed_ref,
    state_ref,
    ncx_ref,
    ncb_ref,
    a_buf,
    w_own,
    w_all,
    d_all,
    wxz,
    xz_send,
    xz_recv,
    z_own,
    z_all,
    head_buf,
    s_bc,
    cc_own,
    cc_all,
    q_buf,
    cum_buf,
    w5,
    terms,
    p_send,
    p_recv,
    s_x,
    xs_buf,
    bs_buf,
    g_own,
    g_all,
    w_ext,
    f_send,
    f_recv,
    send_sem,
    recv_sem,
):
    me = lax.axis_index("req")
    mf = lax.axis_index("fsdp")
    ks, inner = xw_ref.shape
    half = ks // 2
    heads = dtw_ref.shape[1]
    ns = bcw_ref.shape[1] // 2
    slots = page_x_ref.shape[0]
    page = page_x_ref.shape[1]
    total_inner = inner * F
    ocols = ow_ref.shape[1]
    pad_in = p_send.shape[1]
    mine = lax.div(me, 2)
    is_self = mine == mf

    barrier = pltpu.get_barrier_semaphore()

    @pl.loop(1, R)
    def _(i):
        pl.semaphore_signal(
            barrier, inc=1, device_id={"req": lax.rem(me + i, R)}, device_id_type=MESH
        )

    @pl.loop(1, F)
    def _(i):
        pl.semaphore_signal(
            barrier, inc=1, device_id={"fsdp": lax.rem(mf + i, F)}, device_id_type=MESH
        )

    @pl.loop(0, F)
    def _(i):
        g = lax.rem(mf + i, F)

        @pl.when(jnp.logical_or(g != mf, 2 * mf != me))
        def _():
            pl.semaphore_signal(
                barrier, inc=1, device_id={"req": 2 * mf, "fsdp": g}, device_id_type=MESH
            )

        @pl.when(jnp.logical_or(g != mf, 2 * mf + 1 != me))
        def _():
            pl.semaphore_signal(
                barrier, inc=1, device_id={"req": 2 * mf + 1, "fsdp": g}, device_id_type=MESH
            )

    wpad = jnp.concatenate([bcw_ref[...], jnp.zeros((LN - ks, 2 * ns), bf16)], axis=0)
    pick = (iota((T, 2 * ns), 1) == T * mf + iota((T, 2 * ns), 0)).astype(bf16)
    bc_rows = nt(pick, wpad)
    dpad = jnp.concatenate([dtw_ref[...], jnp.zeros((LN - ks, heads), bf16)], axis=0)
    row5 = iota((T, heads), 0)
    col5 = iota((T, heads), 1)
    pick5 = ((row5 == col5) | (row5 == col5 + heads)).astype(bf16)
    dt_rows = nt(pick5, dpad)
    row = iota((T, LN), 0)
    lane = iota((T, LN), 1)
    dt_rows = jnp.where(
        row < heads, pltpu.roll(dt_rows, ks, 1), pltpu.roll(dt_rows, half, 1)
    )
    dt_zone = (lane >= ks) & (lane < ks + half)
    w_own[...] = jnp.where(
        lane < ks, bc_rows, jnp.where(dt_zone & (row < 2 * heads), dt_rows, 0.0)
    ).astype(bf16)
    w_all[:, pl.ds(pl.multiple_of(me * LN, LN), LN)] = w_own[...]

    a_buf[pl.ds(48, LN - 48), :] = jnp.zeros((LN - 48, R * LN), bf16)
    for j in range(R):
        start = ks * j
        base = start // LN * LN
        off = start - base
        if off + ks <= LN:
            window = drafts_ref[0, :, pl.ds(base, LN)].astype(f32)
            if off:
                window = pltpu.roll(window, LN - off, 1)
        else:
            window = drafts_ref[0, :, pl.ds(base, 2 * LN)].astype(f32)
            window = pltpu.roll(window, 2 * LN - off, 1)[:, :LN]
        a_buf[pl.ds(0, T), pl.ds(LN * j, LN)] = jnp.where(lane < ks, window, 0.0).astype(bf16)
        a_buf[pl.ds(T, T), pl.ds(LN * j, LN)] = jnp.where(
            dt_zone, pltpu.roll(window, ks, 1), 0.0
        ).astype(bf16)
        a_buf[pl.ds(2 * T, T), pl.ds(LN * j, LN)] = jnp.where(
            dt_zone, pltpu.roll(window, half, 1), 0.0
        ).astype(bf16)
    own_rows = pl.ds(pl.multiple_of(me * T, T), T)
    d_all[own_rows, :] = a_buf[pl.ds(0, T), pl.ds(pl.multiple_of(me * LN, LN), LN)]

    pl.semaphore_wait(barrier, (R - 1) + (F - 1) + R - is_self.astype(jnp.int32))

    def put(src, dst, phase, device):
        pltpu.make_async_remote_copy(
            src_ref=src,
            dst_ref=dst,
            send_sem=send_sem.at[phase],
            recv_sem=recv_sem.at[phase],
            device_id=device,
            device_id_type=MESH,
        ).start()

    def wait_bytes(ref, sem):
        pltpu.make_async_copy(ref, ref, sem).wait()

    own_lanes = pl.ds(pl.multiple_of(me * LN, LN), LN)

    @pl.loop(1, R)
    def _(i):
        put(w_own, w_all.at[:, own_lanes], 0, {"req": lax.rem(me + i, R)})

    @pl.loop(1, R)
    def _(i):
        r = lax.rem(me + i, R)
        put(
            a_buf.at[pl.ds(0, T), pl.ds(pl.multiple_of(r * LN, LN), LN)],
            d_all.at[own_rows, :],
            1,
            {"req": r},
        )

    wxz[pl.ds(0, ks), pl.ds(0, inner)] = xw_ref[...]
    wxz[pl.ds(0, ks), pl.ds(inner, inner)] = zw_ref[...]
    wxz[pl.ds(ks, LN - ks), :] = jnp.zeros((LN - ks, 2 * inner), bf16)
    head_buf[...] = jnp.zeros(head_buf.shape, f32)
    head_buf[pl.ds(0, 1), pl.ds(0, heads)] = dt_bias_ref[...]
    head_buf[pl.ds(1, 1), pl.ds(0, heads)] = decay_ref[...]
    s_bc[...] = jnp.zeros(s_bc.shape, f32)
    s_bc[pl.ds(T - KC + 1, KC - 1), :] = cbs_ref[0].astype(f32)
    s_x[...] = jnp.zeros(s_x.shape, f32)
    s_x[pl.ds(T - KC + 1, KC - 1), :] = cxs_ref[0].astype(f32)
    bs_buf[...] = jnp.zeros(bs_buf.shape, f32)
    bs_buf[pl.ds(T, 4), :] = sink_b_ref[0].astype(f32)
    xs_buf[...] = jnp.zeros(xs_buf.shape, f32)
    xs_buf[pl.ds(T, 4), :] = sink_x_ref[0].astype(f32)
    w_ext[...] = jnp.zeros(w_ext.shape, bf16)
    w_ext[pl.ds(0, inner), pl.ds(0, ocols)] = ow_ref[...]
    tail = pad_in - inner
    er = iota((tail, LN), 0)
    el = iota((tail, LN), 1)
    w_ext[pl.ds(inner, tail), :] = jnp.where(
        (el >= ocols) & (el < ocols + 3) & (el - ocols == er), 1.0, w_ext[pl.ds(inner, tail), :].astype(f32)
    ).astype(bf16)

    rows_of = []
    live_of = []
    for s in range(slots):
        req = slot_req_ref[s]
        guarded = jnp.maximum(req, 0)
        live_of.append((req >= 0) & (slot_page_ref[s] < page_count_ref[guarded]))
        rows_of.append(owner_row_ref[guarded])
    by_sub = jnp.zeros((slots * T, 1), jnp.int32)
    by_lane = jnp.zeros((1, slots * T), jnp.int32)
    live_sub = jnp.zeros((slots * T, 1), jnp.int32)
    for s in range(slots):
        in_sub = lax.div(iota((slots * T, 1), 0), T) == s
        in_lane = lax.div(iota((1, slots * T), 1), T) == s
        by_sub = jnp.where(in_sub, T * (rows_of[s] - s), by_sub)
        live_sub = jnp.where(in_sub, live_of[s].astype(jnp.int32), live_sub)
        by_lane = jnp.where(
            in_lane, jnp.where(live_of[s], T * (rows_of[s] - s), -(1 << 20)), by_lane
        )
    gather_rows = (
        iota((slots * T, R * T), 1) == iota((slots * T, R * T), 0) + by_sub
    ).astype(bf16)
    scatter_rows = (
        iota((R * T, slots * T), 0) == iota((R * T, slots * T), 1) + by_lane
    ).astype(bf16)

    wait_bytes(w_all.at[:, pl.ds(0, (R - 1) * LN)], recv_sem.at[0])
    proj = nt(a_buf[...], w_all[...])
    z_own[...] = nt((iota((T, T), 0) == iota((T, T), 1)).astype(bf16), proj.astype(bf16)).astype(bf16)
    z_rows = pl.ds(pl.multiple_of(mf * T, T), T)
    z_all[z_rows, :] = z_own[...]

    @pl.loop(1, F)
    def _(i):
        put(z_own, z_all.at[z_rows, :], 2, {"fsdp": lax.rem(mf + i, F)})

    er = iota((T, LN), 0)
    el = iota((T, LN), 1)
    first = ((er == el) & (el < heads)).astype(f32)
    second = ((er == el + heads) & (el < heads)).astype(f32)
    dt_raw = jnp.dot(proj[T : 2 * T], first, precision=EXACT, preferred_element_type=f32) + jnp.dot(
        proj[2 * T : 3 * T], second, precision=EXACT, preferred_element_type=f32
    )
    v = dt_raw + head_buf[pl.ds(0, 1), :]
    dtime = jnp.maximum(v, 0.0) + jnp.log1p(jnp.exp(-jnp.abs(v)))
    upto = (iota((T, T), 1) <= iota((T, T), 0)).astype(f32)
    cumul = -jnp.dot(
        upto, dtime * head_buf[pl.ds(1, 1), :], precision=EXACT, preferred_element_type=f32
    )
    hi, mid, low = pieces3(cumul)
    packed = hi + pltpu.roll(mid, 16, 1) + pltpu.roll(low, 32, 1)

    wait_bytes(z_all.at[pl.ds(0, (F - 1) * T), :], recv_sem.at[2])
    bc_raw = nt((iota((T, LN), 0) == iota((T, LN), 1)).astype(bf16), z_all[...])
    s_bc[pl.ds(T, T), :] = bc_raw
    acc = jnp.zeros((T, 2 * ns), f32) + cbb_ref[...].astype(f32)
    for k in range(KC):
        acc = acc + cbw_ref[pl.ds(k, 1), :].astype(f32) * s_bc[pl.ds(T - KC + 1 + k, T), :]
    bc_act = silu(acc)
    b_mat = bc_act[:, :ns].astype(bf16)
    c_mat = bc_act[:, ns:].astype(bf16)
    cc_own[:, pl.ds(0, ns)] = c_mat
    cc_own[:, pl.ds(ns, LN)] = packed.astype(bf16)
    cc_all[own_rows, :] = cc_own[...]

    @pl.loop(1, R)
    def _(i):
        put(cc_own, cc_all.at[own_rows, :], 3, {"req": lax.rem(me + i, R)})

    wait_bytes(d_all.at[pl.ds(0, (R - 1) * T), :], recv_sem.at[1])
    xz_send[...] = jnp.dot(d_all[...], wxz[...], preferred_element_type=f32).astype(bf16)
    xz_recv[me] = xz_send[own_rows, :]

    @pl.loop(1, R)
    def _(i):
        r = lax.rem(me + i, R)
        put(
            xz_send.at[pl.ds(pl.multiple_of(r * T, T), T), :], xz_recv.at[me], 4, {"req": r}
        )

    head_lane = lax.div(iota((T, inner), 1), HD)

    def own_heads(stacked):
        out = jnp.where(head_lane == 0, stacked[0:T], 0.0)
        for h in range(1, heads):
            out = jnp.where(head_lane == h, stacked[h * T : (h + 1) * T], out)
        return out

    wait_bytes(cc_all.at[pl.ds(0, (R - 1) * T), :], recv_sem.at[3])
    picked = jnp.dot(gather_rows, cc_all[...], preferred_element_type=f32)
    q_buf[...] = picked[:, :ns].astype(bf16)
    cum3 = picked[:, ns:]
    cum_buf[...] = cum3 + pltpu.roll(cum3, LN - 16, 1) + pltpu.roll(cum3, LN - 32, 1)

    @pl.loop(0, slots)
    def _(s):
        rows = pl.ds(pl.multiple_of(s * T, T), T)
        scores = nt(q_buf[rows, :], page_b_ref[s])
        cum = cum_buf[rows, :]
        decays = page_decay_ref[s]
        for h in range(heads):
            factor = jnp.exp(cum[:, h : h + 1] - decays[h : h + 1, :])
            w5[pl.ds(h * T, T), :] = (scores * factor).astype(bf16)
        stacked = jnp.dot(w5[...], page_x_ref[s], preferred_element_type=f32)
        terms[rows, :] = own_heads(stacked)

    kept_terms = jnp.where(live_sub != 0, terms[...], 0.0).astype(bf16)
    summed = jnp.dot(scatter_rows, kept_terms, preferred_element_type=f32)
    p_send[:, pl.ds(0, inner)] = summed.astype(bf16)
    p_send[:, pl.ds(inner, tail)] = jnp.zeros((R * T, tail), bf16)
    p_recv[me] = p_send[own_rows, :]

    @pl.loop(1, R)
    def _(i):
        r = lax.rem(me + i, R)
        put(p_send.at[pl.ds(pl.multiple_of(r * T, T), T), :], p_recv.at[me], 5, {"req": r})

    wait_bytes(xz_recv.at[pl.ds(0, R - 1)], recv_sem.at[4])
    xz = lax.fori_loop(
        1, R, lambda i, total: total + xz_recv[i].astype(f32), xz_recv[0].astype(f32)
    )
    x_raw = xz[:, :inner].astype(bf16).astype(f32)
    z_raw = xz[:, inner:].astype(bf16).astype(f32)
    s_x[pl.ds(T, T), :] = x_raw
    acc = jnp.zeros((T, inner), f32) + cxb_ref[...].astype(f32)
    for k in range(KC):
        acc = acc + cxw_ref[pl.ds(k, 1), :].astype(f32) * s_x[pl.ds(T - KC + 1 + k, T), :]
    x_act = silu(acc).astype(bf16).astype(f32)
    xs_buf[pl.ds(0, T), :] = x_act
    bs_buf[pl.ds(0, T), :] = b_mat.astype(f32)
    scores = nt(c_mat, bs_buf[...].astype(bf16))
    zeros_t = jnp.zeros((T, LN), f32)
    eye8 = (iota((8, LN), 0) == iota((8, LN), 1)).astype(f32)
    cumul_t = nt(eye8, jnp.concatenate([cumul, zeros_t], axis=0), EXACT)
    dtime_t = nt(eye8, jnp.concatenate([dtime, zeros_t], axis=0), EXACT)
    at = iota((T, 2 * T), 0)
    au = iota((T, 2 * T), 1)
    for h in range(heads):
        spread = jnp.where(au <= at, cumul[:, h : h + 1] - cumul_t[h : h + 1, :], 0.0)
        factor = jnp.exp(spread) * dtime_t[h : h + 1, :]
        factor = jnp.where(au >= T, 1.0, jnp.where(au <= at, factor, 0.0))
        w5[pl.ds(h * T, T), pl.ds(0, 2 * T)] = (scores * factor).astype(bf16)
    local = own_heads(
        jnp.dot(
            w5[:, pl.ds(0, 2 * T)], xs_buf[...].astype(bf16), preferred_element_type=f32
        )
    )

    taken = accepted_ref[0]
    at = iota((T, LN), 0)
    last = jnp.sum(jnp.where(at == taken - 1, cumul, 0.0), axis=0, keepdims=True)
    spread = jnp.where(at < taken, last - cumul, 0.0)
    coeff = jnp.where(at < taken, jnp.exp(spread) * dtime, 0.0)
    coeff_x = jnp.zeros((T, inner), f32)
    for h in range(heads):
        coeff_x = jnp.where(head_lane == h, coeff[:, h : h + 1], coeff_x)
    y = coeff_x * x_act
    y_hi = y.astype(bf16).astype(f32)
    y2 = jnp.concatenate([y_hi, y - y_hi], axis=0).astype(bf16)
    b2 = jnp.concatenate([b_mat, b_mat], axis=0)
    fresh = lax.dot_general(
        y2, b2, (((0,), (0,)), ((), ())), preferred_element_type=f32
    )
    keep = jnp.exp(last)
    for h in range(heads):
        state_ref[0, h] = keep[:, h : h + 1] * ssm_ref[0, h] + fresh[h * HD : (h + 1) * HD]
    tail_pick = (
        iota((8, 2 * T), 1) == T - KC + 1 + taken + iota((8, 2 * T), 0)
    ).astype(bf16)
    ncx = jnp.dot(tail_pick, s_x[...].astype(bf16), preferred_element_type=f32)
    ncx_ref[0] = ncx[: KC - 1].astype(bf16)
    ncb = jnp.dot(tail_pick, s_bc[...].astype(bf16), preferred_element_type=f32)
    ncb_ref[0] = ncb[: KC - 1].astype(bf16)
    gate = silu(z_raw)

    wait_bytes(p_recv.at[pl.ds(0, R - 1)], recv_sem.at[5])
    page_sum = lax.fori_loop(
        1, R, lambda i, total: total + p_recv[i].astype(f32), p_recv[0].astype(f32)
    )[:, :inner]
    gated = (page_sum + local) * gate
    squares = jnp.sum(gated * gated, axis=1, keepdims=True)
    hi, mid, low = pieces3(squares)
    el = iota((T, tail), 1)
    g_own[:, pl.ds(0, inner)] = (gated * gain_ref[...].astype(f32)).astype(bf16)
    g_own[:, pl.ds(inner, tail)] = jnp.where(
        el == 0, hi, jnp.where(el == 1, mid, jnp.where(el == 2, low, 0.0))
    ).astype(bf16)
    g_all[own_rows, :] = g_own[...]

    @pl.loop(1, R)
    def _(i):
        put(g_own, g_all.at[own_rows, :], 6, {"req": lax.rem(me + i, R)})

    wait_bytes(g_all.at[pl.ds(0, (R - 1) * T), :], recv_sem.at[6])
    f_send[...] = jnp.dot(g_all[...], w_ext[...], preferred_element_type=f32).astype(bf16)
    slot = lax.rem(me, 2) * F + mf

    @pl.when(is_self)
    def _():
        f_recv[slot] = f_send[own_rows, :]

    @pl.when(jnp.logical_not(is_self))
    def _():
        put(f_send.at[own_rows, :], f_recv.at[slot], 7, {"req": me, "fsdp": mine})

    @pl.loop(1, R)
    def _(i):
        r = lax.rem(me + i, R)
        put(
            f_send.at[pl.ds(pl.multiple_of(r * T, T), T), :],
            f_recv.at[slot],
            7,
            {"req": r, "fsdp": mine},
        )

    @pl.when(is_self)
    def _():
        wait_bytes(f_recv.at[pl.ds(0, R - 1)], recv_sem.at[7])

    @pl.when(jnp.logical_not(is_self))
    def _():
        wait_bytes(f_recv, recv_sem.at[7])

    even = lax.fori_loop(
        1, F, lambda i, total: total + f_recv[i].astype(f32), f_recv[0].astype(f32)
    )
    odd = lax.fori_loop(
        1, F, lambda i, total: total + f_recv[F + i].astype(f32), f_recv[F].astype(f32)
    )
    total_squares = (
        even[:, ocols : ocols + 1]
        + even[:, ocols + 1 : ocols + 2]
        + even[:, ocols + 2 : ocols + 3]
    )
    scale = lax.rsqrt(total_squares / total_inner + EPSILON)
    moved = pltpu.roll(odd, ocols, 1)
    mixed_ref[0, :, pl.ds(0, LN)] = (jnp.where(lane < ocols, even, moved) * scale).astype(bf16)
    mixed_ref[0, :, pl.ds(LN, 2 * ocols - LN)] = (moved * scale)[:, : 2 * ocols - LN].astype(bf16)

    wait_bytes(w_all.at[:, pl.ds(0, (R - 1) * LN)], send_sem.at[0])
    wait_bytes(d_all.at[pl.ds(0, (R - 1) * T), :], send_sem.at[1])
    wait_bytes(z_all.at[pl.ds(0, (F - 1) * T), :], send_sem.at[2])
    wait_bytes(cc_all.at[pl.ds(0, (R - 1) * T), :], send_sem.at[3])
    wait_bytes(xz_recv.at[pl.ds(0, R - 1)], send_sem.at[4])
    wait_bytes(p_recv.at[pl.ds(0, R - 1)], send_sem.at[5])
    wait_bytes(g_all.at[pl.ds(0, (R - 1) * T), :], send_sem.at[6])

    @pl.when(is_self)
    def _():
        wait_bytes(f_recv.at[pl.ds(0, R - 1)], send_sem.at[7])

    @pl.when(jnp.logical_not(is_self))
    def _():
        wait_bytes(f_recv, send_sem.at[7])


def per_device(
    R,
    F,
    drafts,
    x_weight,
    z_weight,
    bc_weight,
    dt_weight,
    dt_bias,
    decay_rate,
    conv_x_weight,
    conv_x_bias,
    conv_bc_weight,
    conv_bc_bias,
    norm_gain,
    out_weight,
    conv_x_state,
    conv_bc_state,
    ssm_state,
    sink_x,
    sink_b,
    page_x,
    page_b,
    page_decay,
    slot_req,
    slot_page,
    page_count,
    accepted,
    owner_row,
):
    inner = x_weight.shape[1]
    ns = bc_weight.shape[1] // 2
    slots, page, _ = page_x.shape
    heads = dt_weight.shape[1]
    ocols = out_weight.shape[1]
    pad_in = -(-inner // LN) * LN
    vmem = pl.BlockSpec(memory_space=pltpu.VMEM)
    smem = pl.BlockSpec(memory_space=pltpu.SMEM)
    shape = jax.ShapeDtypeStruct
    scratch = [
        pltpu.VMEM((LN, R * LN), bf16),
        pltpu.VMEM((T, LN), bf16),
        pltpu.VMEM((T, R * LN), bf16),
        pltpu.VMEM((R * T, LN), bf16),
        pltpu.VMEM((LN, 2 * inner), bf16),
        pltpu.VMEM((R * T, 2 * inner), bf16),
        pltpu.VMEM((R, T, 2 * inner), bf16),
        pltpu.VMEM((T, LN), bf16),
        pltpu.VMEM((F * T, LN), bf16),
        pltpu.VMEM((8, LN), f32),
        pltpu.VMEM((2 * T, 2 * ns), f32),
        pltpu.VMEM((T, ns + LN), bf16),
        pltpu.VMEM((R * T, ns + LN), bf16),
        pltpu.VMEM((slots * T, ns), bf16),
        pltpu.VMEM((slots * T, LN), f32),
        pltpu.VMEM((heads * T, page), bf16),
        pltpu.VMEM((slots * T, inner), f32),
        pltpu.VMEM((R * T, pad_in), bf16),
        pltpu.VMEM((R, T, pad_in), bf16),
        pltpu.VMEM((2 * T, inner), f32),
        pltpu.VMEM((2 * T, inner), f32),
        pltpu.VMEM((2 * T, ns), f32),
        pltpu.VMEM((T, pad_in), bf16),
        pltpu.VMEM((R * T, pad_in), bf16),
        pltpu.VMEM((pad_in, LN), bf16),
        pltpu.VMEM((R * T, LN), bf16),
        pltpu.VMEM((2 * F, T, LN), bf16),
        pltpu.SemaphoreType.DMA((8,)),
        pltpu.SemaphoreType.DMA((8,)),
    ]
    return pl.pallas_call(
        functools.partial(kernel, R, F),
        out_shape=(
            shape((1, T, 2 * ocols), bf16),
            shape(ssm_state.shape, f32),
            shape(conv_x_state.shape, bf16),
            shape(conv_bc_state.shape, bf16),
        ),
        in_specs=[vmem] * 21 + [smem] * 5,
        out_specs=(vmem,) * 4,
        scratch_shapes=scratch,
        compiler_params=pltpu.CompilerParams(
            collective_id=0, has_side_effects=True, vmem_limit_bytes=48 << 20
        ),
        name="mixer",
    )(
        drafts,
        x_weight,
        z_weight,
        bc_weight,
        dt_weight,
        dt_bias.reshape(1, -1),
        decay_rate.reshape(1, -1),
        conv_x_weight,
        conv_x_bias.reshape(1, -1),
        conv_bc_weight,
        conv_bc_bias.reshape(1, -1),
        norm_gain.reshape(1, -1),
        out_weight,
        conv_x_state,
        conv_bc_state,
        ssm_state,
        sink_x,
        sink_b,
        page_x,
        page_b,
        page_decay,
        slot_req,
        slot_page,
        page_count,
        accepted,
        owner_row,
    )


def solution(mesh):
    in_specs = (
        P("req", None, None),
        P("req", "fsdp"),
        P("req", "fsdp"),
        P("req", None),
        P("req", "fsdp"),
        P("fsdp"),
        P("fsdp"),
        P(None, "fsdp"),
        P("fsdp"),
        P(),
        P(),
        P("fsdp"),
        P("fsdp", "req"),
        P("req", None, "fsdp"),
        P("req", None, None),
        P("req", "fsdp", None, None),
        P("req", None, "fsdp"),
        P("req", None, None),
        P("req", None, "fsdp"),
        P("req", None, None),
        P("req", "fsdp", None),
        P("req"),
        P("req"),
        P(),
        P("req"),
        P(),
    )
    out_specs = (
        P("req", None, "fsdp"),
        P("req", "fsdp", None, None),
        P("req", None, "fsdp"),
        P("req", None, None),
    )
    return jax.shard_map(
        functools.partial(per_device, mesh.shape["req"], mesh.shape["fsdp"]),
        mesh=mesh,
        in_specs=in_specs,
        out_specs=out_specs,
        check_vma=False,
    )
```

time: 643 us -> 96.4 us (0.15)
  waiting for transfers between devices: 469 us -> 0 us
  blocking collectives: 131 us -> 0 us
  Pallas kernels: 0 us -> 85.3 us
  matrix products: 13.8 us -> 0 us
  between operations: 15.1 us -> 1.72 us
    reduce_scatter x1 -> x0, waiting for transfers between devices: 218 us -> none  [per_device(): lax.psum_scatter(partial_value, 'req', scatter_dimension=0, tiled=True)]
    all_gather x4 -> x0, waiting for transfers between devices: 190 us -> none  [the longest x1 81.3 us: per_device(): lax.all_gather(z_weight, 'req', axis=0, tiled=True)]
    all_gather x3 -> x0, blocking collectives: 101 us -> none  [the longest x1 39.1 us: per_device(): lax.all_gather(dt_weight, 'req', axis=0, tiled=True)]
    pallas_call x0 -> x1, Pallas kernels: none -> 85.3 us  [per_device(): pl.pallas_call(functools.partial(kernel, R, F), out_shape=(shape((1, T, 2...]
    unnamed x7 -> x0, waiting for transfers between devices: 61.2 us -> none
    psum x1 -> x0, blocking collectives: 29.8 us -> none  [per_device(): square_sum = lax.psum(jnp.sum(gated * gated, axis=-1), 'fsdp')]
    dot_general x11 -> x0, matrix products: 10.4 us -> none  [the longest x4 6.45 us: per_device(): jnp.dot(flat_tokens, weight_rows, preferred_element_type=jnp.float32)]
  transfers between devices with their start and end apart: 6 -> 0, of which waited for: 6 -> 0; matrix products, arithmetic and copies ran while one was open for 3% -> 0% of each run, Pallas kernels for 0% -> 0%
where the time goes in v1:
time: 96.4 us; the launch traced here: 96.1 us
  Pallas kernels  85.3 us (88%)
  local copies, waits for them, and re-layouts  9 us (9%)
  between operations  1.72 us (2%)
    pallas_call x1, Pallas kernels, per_device(): pl.pallas_call(functools.partial(kernel, R, F), out_shape=(shape((1, T, 2...  85.3 us
    unnamed x45, local copies, waits for them, and re-layouts  6.98 us

profile of v1, /device:TPU:1, one launch (start us, length us, event | category | flops | bytes accessed | tf_op | source)
XLA Modules:
  0.0 96.1 jit_solution(5808404480854707543)
XLA Ops:
  0.6 0.0 copy-start.18
  0.7 0.0 copy-start.17
  0.7 0.0 copy-start.16
  0.7 0.0 copy-start.15
  0.7 0.0 copy-start.3
  0.7 0.0 copy-start
  0.7 0.0 copy-start.12
  0.7 0.0 copy-start.9
  0.7 0.0 copy-start.1
  0.7 0.0 copy-start.11
  0.7 0.0 copy-start.8
  0.8 0.0 copy-start.10
  0.8 0.0 copy-start.7
  0.8 0.0 copy-start.14
  0.8 0.0 copy-start.13
  0.8 0.0 copy-start.6
  0.8 0.0 copy-start.5
  0.8 0.0 copy-start.4
  1.6 0.7 reshape.26.cbb_ref
  2.2 0.7 reshape.25.cxb_ref
  2.9 0.7 reshape.27.gain_ref
  3.6 0.8 copy.30.dtw_ref
  4.4 0.9 copy.31.ow_ref
  5.3 2.7 %copy.32.page_x_ref = bf16[10,256,320]{2,1,0:T(8,128)(2,1)S(1)} copy(bf16[10,256,320]{1,2,0:T(8,128)(2,1)} %param.44) | data formatting | bytes 3276800 | tf_op args[18]
  8.1 0.0 copy-done.18
  8.1 0.0 copy-done.17
  8.1 0.0 copy-done.16
  8.1 0.0 copy-done.15
  8.1 0.0 copy-done.3
  8.1 0.0 copy-done
  8.2 0.0 copy-done.12
  8.2 0.0 copy-done.9
  8.2 0.0 copy-done.1
  8.2 0.0 copy-done.11
  8.2 0.0 copy-done.8
  8.2 0.0 copy-done.10
  8.2 0.0 copy-done.7
  8.2 0.0 copy-done.14
  8.2 0.0 copy-done.13
  8.2 0.0 copy-done.6
  8.3 0.0 copy-done.5
  8.3 0.0 copy-done.4
  8.3 0.0 copy-done.2
  8.3 85.3 %mixer.1 = (bf16[1,16,160]{2,1,0:T(8,128)(2,1)S(1)}, f32[1,5,64,128]{3,2,1,0:T(8,128)S(1)}, bf16[1,3,320]{2,1,0:T(4,128)(2,1)S(1)}, bf16[1,3,256]{2,1,0:T(4,128)(2,1)S(1)}) custom-call(bf16[1,16,2560]{2,1,0:T(8,128)(2,1)S(1)} %copy-done.2, bf16[80,320]{1,0:T(8,128)(2,1)S(1)} %copy-done.4, bf16[80,320]{1,0:T(8,128)(2,1)S(1)} %copy-done.5, ...), custom_call_target="tpu_custom_call" | custom-call | tf_op jit(solution)/shard_map/mixer/pallas_call | solution.py:570
  93.6 0.6 copy.38
  94.2 0.7 copy.39
  94.9 0.6 copy.40
  95.5 0.6 copy.41
  (1 shorter events, 0.0 us)
Async XLA Ops:
  0.6 7.5 %copy-start.18 = (s32[32]{0:T(128)S(1)}, s32[32]{0:T(128)}, u32[]{:S(2)}) copy-start(s32[32]{0:T(128)} %owner_row_ref.1) | copy-start | bytes 388
  0.7 7.5 %copy-start.17 = (s32[32]{0:T(128)S(1)}, s32[32]{0:T(128)}, u32[]{:S(2)}) copy-start(s32[32]{0:T(128)} %page_count_ref.1) | copy-start | bytes 388
  0.7 7.5 %copy-start.16 = (s32[10]{0:T(128)S(1)}, s32[10]{0:T(128)}, u32[]{:S(2)}) copy-start(s32[10]{0:T(128)} %slot_page_ref.1) | copy-start | bytes 124
  0.7 7.5 %copy-start.15 = (s32[10]{0:T(128)S(1)}, s32[10]{0:T(128)}, u32[]{:S(2)}) copy-start(s32[10]{0:T(128)} %slot_req_ref.1) | copy-start | bytes 124
  0.7 7.5 %copy-start.3 = (f32[10,5,256]{2,1,0:T(8,128)S(1)}, f32[10,5,256]{2,1,0:T(8,128)}, u32[]{:S(2)}) copy-start(f32[10,5,256]{2,1,0:T(8,128)} %page_decay_ref.1) | copy-start | bytes 153604
  0.7 7.5 %copy-start = (bf16[10,256,128]{2,1,0:T(8,128)(2,1)S(1)}, bf16[10,256,128]{2,1,0:T(8,128)(2,1)}, u32[]{:S(2)}) copy-start(bf16[10,256,128]{2,1,0:T(8,128)(2,1)} %page_b_ref.1) | copy-start | bytes 1966084
  0.7 7.5 %copy-start.12 = (bf16[1,4,128]{2,1,0:T(4,128)(2,1)S(1)}, bf16[1,4,128]{2,1,0:T(4,128)(2,1)}, u32[]{:S(2)}) copy-start(bf16[1,4,128]{2,1,0:T(4,128)(2,1)} %sink_b_ref.1) | copy-start | bytes 3076
  0.7 7.5 %copy-start.9 = (bf16[1,4,320]{2,1,0:T(4,128)(2,1)S(1)}, bf16[1,4,320]{2,1,0:T(4,128)(2,1)}, u32[]{:S(2)}) copy-start(bf16[1,4,320]{2,1,0:T(4,128)(2,1)} %sink_x_ref.1) | copy-start | bytes 7684
  0.7 7.5 %copy-start.1 = (f32[1,5,64,128]{3,2,1,0:T(8,128)S(1)}, f32[1,5,64,128]{3,2,1,0:T(8,128)}, u32[]{:S(2)}) copy-start(f32[1,5,64,128]{3,2,1,0:T(8,128)} %ssm_ref.1) | copy-start | bytes 491524
  0.7 7.5 %copy-start.11 = (bf16[1,3,256]{2,1,0:T(4,128)(2,1)S(1)}, bf16[1,3,256]{2,1,0:T(4,128)(2,1)}, u32[]{:S(2)}) copy-start(bf16[1,3,256]{2,1,0:T(4,128)(2,1)} %cbs_ref.1) | copy-start | bytes 4612
  0.7 7.5 %copy-start.8 = (bf16[1,3,320]{2,1,0:T(4,128)(2,1)S(1)}, bf16[1,3,320]{2,1,0:T(4,128)(2,1)}, u32[]{:S(2)}) copy-start(bf16[1,3,320]{2,1,0:T(4,128)(2,1)} %cxs_ref.1) | copy-start | bytes 5764
  0.8 7.5 %copy-start.10 = (bf16[4,256]{1,0:T(4,128)(2,1)S(1)}, bf16[4,256]{1,0:T(4,128)(2,1)}, u32[]{:S(2)}) copy-start(bf16[4,256]{1,0:T(4,128)(2,1)} %cbw_ref.1) | copy-start | bytes 6148
  0.8 7.5 %copy-start.7 = (bf16[4,320]{1,0:T(4,128)(2,1)S(1)}, bf16[4,320]{1,0:T(4,128)(2,1)}, u32[]{:S(2)}) copy-start(bf16[4,320]{1,0:T(4,128)(2,1)} %cxw_ref.1) | copy-start | bytes 7684
  0.8 7.5 %copy-start.14 = (f32[5]{0:T(128)S(1)}, f32[5]{0:T(128)}, u32[]{:S(2)}) copy-start(f32[5]{0:T(128)} %param.32) | copy-start | bytes 64
  0.8 7.5 %copy-start.13 = (f32[5]{0:T(128)S(1)}, f32[5]{0:T(128)}, u32[]{:S(2)}) copy-start(f32[5]{0:T(128)} %param.31) | copy-start | bytes 64
  0.8 7.5 %copy-start.6 = (bf16[80,256]{1,0:T(8,128)(2,1)S(1)}, bf16[80,256]{1,0:T(8,128)(2,1)}, u32[]{:S(2)}) copy-start(bf16[80,256]{1,0:T(8,128)(2,1)} %bcw_ref.1) | copy-start | bytes 122884
  0.8 7.5 %copy-start.5 = (bf16[80,320]{1,0:T(8,128)(2,1)S(1)}, bf16[80,320]{1,0:T(8,128)(2,1)}, u32[]{:S(2)}) copy-start(bf16[80,320]{1,0:T(8,128)(2,1)} %zw_ref.1) | copy-start | bytes 153604
  0.8 7.5 %copy-start.4 = (bf16[80,320]{1,0:T(8,128)(2,1)S(1)}, bf16[80,320]{1,0:T(8,128)(2,1)}, u32[]{:S(2)}) copy-start(bf16[80,320]{1,0:T(8,128)(2,1)} %xw_ref.1) | copy-start | bytes 153604
  0.8 7.5 %copy-start.2 = (bf16[1,16,2560]{2,1,0:T(8,128)(2,1)S(1)}, bf16[1,16,2560]{2,1,0:T(8,128)(2,1)}, u32[]{:S(2)}) copy-start(bf16[1,16,2560]{2,1,0:T(8,128)(2,1)} %drafts_ref.1) | copy-start | bytes 245764

commit v2 on v1

--- a/solution.py
+++ b/solution.py
@@ -9,6 +9,7 @@
 
 MESH = pl.DeviceIdType.MESH
 T = 16
+X = 4
 KC = 4
 HD = 64
 LN = 128
@@ -73,6 +74,7 @@
     state_ref,
     ncx_ref,
     ncb_ref,
+    dt_buf,
     a_buf,
     w_own,
     w_all,
@@ -107,15 +109,17 @@
     mf = lax.axis_index("fsdp")
     ks, inner = xw_ref.shape
     half = ks // 2
-    heads = dtw_ref.shape[1]
+    heads = dtw_ref.shape[0]
     ns = bcw_ref.shape[1] // 2
     slots = page_x_ref.shape[0]
-    page = page_x_ref.shape[1]
     total_inner = inner * F
-    ocols = ow_ref.shape[1]
-    pad_in = p_send.shape[1]
-    mine = lax.div(me, 2)
-    is_self = mine == mf
+    ocols = ow_ref.shape[0]
+    pad_in = g_own.shape[1]
+    Y = R // X
+    per_row = X // 2
+    my = lax.div(me, X)
+    mx = lax.rem(me, X)
+    is_self = lax.div(mf, per_row) == my
 
     barrier = pltpu.get_barrier_semaphore()
 
@@ -131,32 +135,27 @@
             barrier, inc=1, device_id={"fsdp": lax.rem(mf + i, F)}, device_id_type=MESH
         )
 
+    source = lax.div(mf, per_row) * X + mx
+
     @pl.loop(0, F)
     def _(i):
         g = lax.rem(mf + i, F)
 
-        @pl.when(jnp.logical_or(g != mf, 2 * mf != me))
+        @pl.when(jnp.logical_or(g != mf, source != me))
         def _():
             pl.semaphore_signal(
-                barrier, inc=1, device_id={"req": 2 * mf, "fsdp": g}, device_id_type=MESH
-            )
-
-        @pl.when(jnp.logical_or(g != mf, 2 * mf + 1 != me))
-        def _():
-            pl.semaphore_signal(
-                barrier, inc=1, device_id={"req": 2 * mf + 1, "fsdp": g}, device_id_type=MESH
+                barrier, inc=1, device_id={"req": source, "fsdp": g}, device_id_type=MESH
             )
 
     wpad = jnp.concatenate([bcw_ref[...], jnp.zeros((LN - ks, 2 * ns), bf16)], axis=0)
     pick = (iota((T, 2 * ns), 1) == T * mf + iota((T, 2 * ns), 0)).astype(bf16)
     bc_rows = nt(pick, wpad)
-    dpad = jnp.concatenate([dtw_ref[...], jnp.zeros((LN - ks, heads), bf16)], axis=0)
-    row5 = iota((T, heads), 0)
-    col5 = iota((T, heads), 1)
-    pick5 = ((row5 == col5) | (row5 == col5 + heads)).astype(bf16)
-    dt_rows = nt(pick5, dpad)
     row = iota((T, LN), 0)
     lane = iota((T, LN), 1)
+    dt_buf[...] = jnp.zeros(dt_buf.shape, f32)
+    dt_buf[pl.ds(0, heads), pl.ds(0, ks)] = dtw_ref[...].astype(f32)
+    dt_buf[pl.ds(heads, heads), pl.ds(0, ks)] = dtw_ref[...].astype(f32)
+    dt_rows = dt_buf[...]
     dt_rows = jnp.where(
         row < heads, pltpu.roll(dt_rows, ks, 1), pltpu.roll(dt_rows, half, 1)
     )
@@ -165,6 +164,57 @@
         lane < ks, bc_rows, jnp.where(dt_zone & (row < 2 * heads), dt_rows, 0.0)
     ).astype(bf16)
     w_all[:, pl.ds(pl.multiple_of(me * LN, LN), LN)] = w_own[...]
+
+    own_rows = pl.ds(pl.multiple_of(me * T, T), T)
+    y_rows = pl.ds(pl.multiple_of(my * T, T), T)
+    pl.semaphore_wait(
+        barrier, (R - 1) + (F - 1) + Y * per_row - is_self.astype(jnp.int32)
+    )
+
+    def put(src, dst, phase, device):
+        pltpu.make_async_remote_copy(
+            src_ref=src,
+            dst_ref=dst,
+            send_sem=send_sem.at[phase],
+            recv_sem=recv_sem.at[phase],
+            device_id=device,
+            device_id_type=MESH,
+        ).start()
+
+    def wait_bytes(ref, sem):
+        pltpu.make_async_copy(ref, ref, sem).wait()
+
+    own_lanes = pl.ds(pl.multiple_of(me * LN, LN), LN)
+    w_bytes = wxz.at[pl.ds(0, (X - 1) * ks), :]
+    o_bytes = w_ext.at[pl.ds(0, (X - 1) * ocols), :]
+
+    @pl.loop(1, R)
+    def _(i):
+        put(w_own, w_all.at[:, own_lanes], 0, {"req": lax.rem(me + i, R)})
+
+    own_block = pl.ds(pl.multiple_of(mx * LN, LN), ks)
+    own_outs = pl.ds(
+        pl.multiple_of(lax.div(mx, 2) * 2 * LN + lax.rem(mx, 2) * ocols, 16), ocols
+    )
+    tail = pad_in - inner
+    for i in range(X):
+        wxz[pl.ds(LN * i + ks, LN - ks), :] = jnp.zeros((LN - ks, 2 * inner), bf16)
+    wxz[own_block, pl.ds(0, inner)] = xw_ref[...]
+    wxz[own_block, pl.ds(inner, inner)] = zw_ref[...]
+    w_ext[own_outs, pl.ds(0, inner)] = ow_ref[...]
+    w_ext[own_outs, pl.ds(inner, tail)] = jnp.zeros((ocols, tail), bf16)
+    rest = 2 * LN - 2 * ocols
+    er = iota((rest, tail), 0)
+    el = iota((rest, tail), 1)
+    for i in range(per_row):
+        top = pl.ds(2 * LN * i + 2 * ocols, rest)
+        w_ext[top, pl.ds(0, inner)] = jnp.zeros((rest, inner), bf16)
+        w_ext[top, pl.ds(inner, tail)] = ((er == el) & (el < 3)).astype(bf16)
+
+    @pl.loop(1, X)
+    def _(i):
+        r = my * X + lax.rem(mx + i, X)
+        put(wxz.at[own_block, :], wxz.at[own_block, :], 8, {"req": r})
 
     a_buf[pl.ds(48, LN - 48), :] = jnp.zeros((LN - 48, R * LN), bf16)
     for j in range(R):
@@ -185,43 +235,23 @@
         a_buf[pl.ds(2 * T, T), pl.ds(LN * j, LN)] = jnp.where(
             dt_zone, pltpu.roll(window, half, 1), 0.0
         ).astype(bf16)
-    own_rows = pl.ds(pl.multiple_of(me * T, T), T)
-    d_all[own_rows, :] = a_buf[pl.ds(0, T), pl.ds(pl.multiple_of(me * LN, LN), LN)]
-
-    pl.semaphore_wait(barrier, (R - 1) + (F - 1) + R - is_self.astype(jnp.int32))
-
-    def put(src, dst, phase, device):
-        pltpu.make_async_remote_copy(
-            src_ref=src,
-            dst_ref=dst,
-            send_sem=send_sem.at[phase],
-            recv_sem=recv_sem.at[phase],
-            device_id=device,
-            device_id_type=MESH,
-        ).start()
-
-    def wait_bytes(ref, sem):
-        pltpu.make_async_copy(ref, ref, sem).wait()
-
-    own_lanes = pl.ds(pl.multiple_of(me * LN, LN), LN)
-
-    @pl.loop(1, R)
-    def _(i):
-        put(w_own, w_all.at[:, own_lanes], 0, {"req": lax.rem(me + i, R)})
-
-    @pl.loop(1, R)
-    def _(i):
-        r = lax.rem(me + i, R)
+    d_all[y_rows, :] = a_buf[pl.ds(0, T), pl.ds(pl.multiple_of(my * X * LN, X * LN), X * LN)]
+
+    @pl.loop(1, Y)
+    def _(i):
+        yy = lax.rem(my + i, Y)
         put(
-            a_buf.at[pl.ds(0, T), pl.ds(pl.multiple_of(r * LN, LN), LN)],
-            d_all.at[own_rows, :],
+            a_buf.at[pl.ds(0, T), pl.ds(pl.multiple_of(yy * X * LN, X * LN), X * LN)],
+            d_all.at[y_rows, :],
             1,
-            {"req": r},
+            {"req": yy * X + mx},
         )
 
-    wxz[pl.ds(0, ks), pl.ds(0, inner)] = xw_ref[...]
-    wxz[pl.ds(0, ks), pl.ds(inner, inner)] = zw_ref[...]
-    wxz[pl.ds(ks, LN - ks), :] = jnp.zeros((LN - ks, 2 * inner), bf16)
+    @pl.loop(1, X)
+    def _(i):
+        r = my * X + lax.rem(mx + i, X)
+        put(w_ext.at[own_outs, :], w_ext.at[own_outs, :], 9, {"req": r})
+
     head_buf[...] = jnp.zeros(head_buf.shape, f32)
     head_buf[pl.ds(0, 1), pl.ds(0, heads)] = dt_bias_ref[...]
     head_buf[pl.ds(1, 1), pl.ds(0, heads)] = decay_ref[...]
@@ -233,15 +263,6 @@
     bs_buf[pl.ds(T, 4), :] = sink_b_ref[0].astype(f32)
     xs_buf[...] = jnp.zeros(xs_buf.shape, f32)
     xs_buf[pl.ds(T, 4), :] = sink_x_ref[0].astype(f32)
-    w_ext[...] = jnp.zeros(w_ext.shape, bf16)
-    w_ext[pl.ds(0, inner), pl.ds(0, ocols)] = ow_ref[...]
-    tail = pad_in - inner
-    er = iota((tail, LN), 0)
-    el = iota((tail, LN), 1)
-    w_ext[pl.ds(inner, tail), :] = jnp.where(
-        (el >= ocols) & (el < ocols + 3) & (el - ocols == er), 1.0, w_ext[pl.ds(inner, tail), :].astype(f32)
-    ).astype(bf16)
-
     rows_of = []
     live_of = []
     for s in range(slots):
@@ -296,7 +317,7 @@
     wait_bytes(z_all.at[pl.ds(0, (F - 1) * T), :], recv_sem.at[2])
     bc_raw = nt((iota((T, LN), 0) == iota((T, LN), 1)).astype(bf16), z_all[...])
     s_bc[pl.ds(T, T), :] = bc_raw
-    acc = jnp.zeros((T, 2 * ns), f32) + cbb_ref[...].astype(f32)
+    acc = jnp.zeros((T, 2 * ns), f32) + cbb_ref[...].astype(f32).reshape(1, 2 * ns)
     for k in range(KC):
         acc = acc + cbw_ref[pl.ds(k, 1), :].astype(f32) * s_bc[pl.ds(T - KC + 1 + k, T), :]
     bc_act = silu(acc)
@@ -310,15 +331,19 @@
     def _(i):
         put(cc_own, cc_all.at[own_rows, :], 3, {"req": lax.rem(me + i, R)})
 
-    wait_bytes(d_all.at[pl.ds(0, (R - 1) * T), :], recv_sem.at[1])
+    wait_bytes(d_all.at[pl.ds(0, (Y - 1) * T), :], recv_sem.at[1])
+    wait_bytes(w_bytes, recv_sem.at[8])
     xz_send[...] = jnp.dot(d_all[...], wxz[...], preferred_element_type=f32).astype(bf16)
-    xz_recv[me] = xz_send[own_rows, :]
-
-    @pl.loop(1, R)
-    def _(i):
-        r = lax.rem(me + i, R)
+    xz_recv[my] = xz_send[y_rows, :]
+
+    @pl.loop(1, Y)
+    def _(i):
+        yy = lax.rem(my + i, Y)
         put(
-            xz_send.at[pl.ds(pl.multiple_of(r * T, T), T), :], xz_recv.at[me], 4, {"req": r}
+            xz_send.at[pl.ds(pl.multiple_of(yy * T, T), T), :],
+            xz_recv.at[my],
+            4,
+            {"req": yy * X + mx},
         )
 
     head_lane = lax.div(iota((T, inner), 1), HD)
@@ -344,7 +369,7 @@
         for h in range(heads):
             factor = jnp.exp(cum[:, h : h + 1] - decays[h : h + 1, :])
             w5[pl.ds(h * T, T), :] = (scores * factor).astype(bf16)
-        stacked = jnp.dot(w5[...], page_x_ref[s], preferred_element_type=f32)
+        stacked = nt(w5[...], page_x_ref[s])
         terms[rows, :] = own_heads(stacked)
 
     kept_terms = jnp.where(live_sub != 0, terms[...], 0.0).astype(bf16)
@@ -358,14 +383,14 @@
         r = lax.rem(me + i, R)
         put(p_send.at[pl.ds(pl.multiple_of(r * T, T), T), :], p_recv.at[me], 5, {"req": r})
 
-    wait_bytes(xz_recv.at[pl.ds(0, R - 1)], recv_sem.at[4])
+    wait_bytes(xz_recv.at[pl.ds(0, Y - 1)], recv_sem.at[4])
     xz = lax.fori_loop(
-        1, R, lambda i, total: total + xz_recv[i].astype(f32), xz_recv[0].astype(f32)
+        1, Y, lambda i, total: total + xz_recv[i].astype(f32), xz_recv[0].astype(f32)
     )
     x_raw = xz[:, :inner].astype(bf16).astype(f32)
     z_raw = xz[:, inner:].astype(bf16).astype(f32)
     s_x[pl.ds(T, T), :] = x_raw
-    acc = jnp.zeros((T, inner), f32) + cxb_ref[...].astype(f32)
+    acc = jnp.zeros((T, inner), f32) + cxb_ref[...].astype(f32).reshape(1, inner)
     for k in range(KC):
         acc = acc + cxw_ref[pl.ds(k, 1), :].astype(f32) * s_x[pl.ds(T - KC + 1 + k, T), :]
     x_act = silu(acc).astype(bf16).astype(f32)
@@ -424,73 +449,73 @@
     squares = jnp.sum(gated * gated, axis=1, keepdims=True)
     hi, mid, low = pieces3(squares)
     el = iota((T, tail), 1)
-    g_own[:, pl.ds(0, inner)] = (gated * gain_ref[...].astype(f32)).astype(bf16)
+    g_own[:, pl.ds(0, inner)] = (gated * gain_ref[...].astype(f32).reshape(1, inner)).astype(bf16)
     g_own[:, pl.ds(inner, tail)] = jnp.where(
         el == 0, hi, jnp.where(el == 1, mid, jnp.where(el == 2, low, 0.0))
     ).astype(bf16)
-    g_all[own_rows, :] = g_own[...]
-
-    @pl.loop(1, R)
-    def _(i):
-        put(g_own, g_all.at[own_rows, :], 6, {"req": lax.rem(me + i, R)})
-
-    wait_bytes(g_all.at[pl.ds(0, (R - 1) * T), :], recv_sem.at[6])
-    f_send[...] = jnp.dot(g_all[...], w_ext[...], preferred_element_type=f32).astype(bf16)
-    slot = lax.rem(me, 2) * F + mf
+    g_all[y_rows, :] = g_own[...]
+
+    @pl.loop(1, Y)
+    def _(i):
+        put(g_own, g_all.at[y_rows, :], 6, {"req": lax.rem(my + i, Y) * X + mx})
+
+    wait_bytes(o_bytes, recv_sem.at[9])
+    wait_bytes(g_all.at[pl.ds(0, (Y - 1) * T), :], recv_sem.at[6])
+    f_send[...] = nt(g_all[...], w_ext[...]).astype(bf16)
+
+    for b in range(per_row):
+        lanes = pl.ds(2 * LN * b, 2 * LN)
+        target = per_row * my + b
+
+        @pl.when(target == mf)
+        def _():
+            f_recv[mf] = f_send[y_rows, lanes]
+
+        @pl.when(target != mf)
+        def _():
+            put(f_send.at[y_rows, lanes], f_recv.at[mf], 7, {"fsdp": target})
+
+        @pl.loop(1, Y)
+        def _(i):
+            yy = lax.rem(my + i, Y)
+            put(
+                f_send.at[pl.ds(pl.multiple_of(yy * T, T), T), lanes],
+                f_recv.at[mf],
+                7,
+                {"req": yy * X + mx, "fsdp": target},
+            )
 
     @pl.when(is_self)
     def _():
-        f_recv[slot] = f_send[own_rows, :]
-
-    @pl.when(jnp.logical_not(is_self))
-    def _():
-        put(f_send.at[own_rows, :], f_recv.at[slot], 7, {"req": me, "fsdp": mine})
-
-    @pl.loop(1, R)
-    def _(i):
-        r = lax.rem(me + i, R)
-        put(
-            f_send.at[pl.ds(pl.multiple_of(r * T, T), T), :],
-            f_recv.at[slot],
-            7,
-            {"req": r, "fsdp": mine},
-        )
-
-    @pl.when(is_self)
-    def _():
-        wait_bytes(f_recv.at[pl.ds(0, R - 1)], recv_sem.at[7])
+        wait_bytes(f_recv.at[pl.ds(0, F - 1)], recv_sem.at[7])
 
     @pl.when(jnp.logical_not(is_self))
     def _():
         wait_bytes(f_recv, recv_sem.at[7])
 
-    even = lax.fori_loop(
+    out = lax.fori_loop(
         1, F, lambda i, total: total + f_recv[i].astype(f32), f_recv[0].astype(f32)
     )
-    odd = lax.fori_loop(
-        1, F, lambda i, total: total + f_recv[F + i].astype(f32), f_recv[F].astype(f32)
-    )
+    wide = 2 * ocols
     total_squares = (
-        even[:, ocols : ocols + 1]
-        + even[:, ocols + 1 : ocols + 2]
-        + even[:, ocols + 2 : ocols + 3]
+        out[:, wide : wide + 1] + out[:, wide + 1 : wide + 2] + out[:, wide + 2 : wide + 3]
     )
     scale = lax.rsqrt(total_squares / total_inner + EPSILON)
-    moved = pltpu.roll(odd, ocols, 1)
-    mixed_ref[0, :, pl.ds(0, LN)] = (jnp.where(lane < ocols, even, moved) * scale).astype(bf16)
-    mixed_ref[0, :, pl.ds(LN, 2 * ocols - LN)] = (moved * scale)[:, : 2 * ocols - LN].astype(bf16)
+    mixed_ref[0] = (out * scale)[:, :wide].astype(bf16)
 
     wait_bytes(w_all.at[:, pl.ds(0, (R - 1) * LN)], send_sem.at[0])
-    wait_bytes(d_all.at[pl.ds(0, (R - 1) * T), :], send_sem.at[1])
+    wait_bytes(d_all.at[pl.ds(0, (Y - 1) * T), :], send_sem.at[1])
     wait_bytes(z_all.at[pl.ds(0, (F - 1) * T), :], send_sem.at[2])
     wait_bytes(cc_all.at[pl.ds(0, (R - 1) * T), :], send_sem.at[3])
-    wait_bytes(xz_recv.at[pl.ds(0, R - 1)], send_sem.at[4])
+    wait_bytes(xz_recv.at[pl.ds(0, Y - 1)], send_sem.at[4])
+    wait_bytes(w_bytes, send_sem.at[8])
+    wait_bytes(o_bytes, send_sem.at[9])
     wait_bytes(p_recv.at[pl.ds(0, R - 1)], send_sem.at[5])
-    wait_bytes(g_all.at[pl.ds(0, (R - 1) * T), :], send_sem.at[6])
+    wait_bytes(g_all.at[pl.ds(0, (Y - 1) * T), :], send_sem.at[6])
 
     @pl.when(is_self)
     def _():
-        wait_bytes(f_recv.at[pl.ds(0, R - 1)], send_sem.at[7])
+        wait_bytes(f_recv.at[pl.ds(0, F - 1)], send_sem.at[7])
 
     @pl.when(jnp.logical_not(is_self))
     def _():
@@ -533,17 +558,19 @@
     heads = dt_weight.shape[1]
     ocols = out_weight.shape[1]
     pad_in = -(-inner // LN) * LN
+    Y = R // X
     vmem = pl.BlockSpec(memory_space=pltpu.VMEM)
     smem = pl.BlockSpec(memory_space=pltpu.SMEM)
     shape = jax.ShapeDtypeStruct
     scratch = [
+        pltpu.VMEM((T, LN), f32),
         pltpu.VMEM((LN, R * LN), bf16),
         pltpu.VMEM((T, LN), bf16),
         pltpu.VMEM((T, R * LN), bf16),
-        pltpu.VMEM((R * T, LN), bf16),
-        pltpu.VMEM((LN, 2 * inner), bf16),
-        pltpu.VMEM((R * T, 2 * inner), bf16),
-        pltpu.VMEM((R, T, 2 * inner), bf16),
+        pltpu.VMEM((Y * T, X * LN), bf16),
+        pltpu.VMEM((X * LN, 2 * inner), bf16),
+        pltpu.VMEM((Y * T, 2 * inner), bf16),
+        pltpu.VMEM((Y, T, 2 * inner), bf16),
         pltpu.VMEM((T, LN), bf16),
         pltpu.VMEM((F * T, LN), bf16),
         pltpu.VMEM((8, LN), f32),
@@ -560,12 +587,12 @@
         pltpu.VMEM((2 * T, inner), f32),
         pltpu.VMEM((2 * T, ns), f32),
         pltpu.VMEM((T, pad_in), bf16),
-        pltpu.VMEM((R * T, pad_in), bf16),
-        pltpu.VMEM((pad_in, LN), bf16),
-        pltpu.VMEM((R * T, LN), bf16),
-        pltpu.VMEM((2 * F, T, LN), bf16),
-        pltpu.SemaphoreType.DMA((8,)),
-        pltpu.SemaphoreType.DMA((8,)),
+        pltpu.VMEM((Y * T, pad_in), bf16),
+        pltpu.VMEM((X * LN, pad_in), bf16),
+        pltpu.VMEM((Y * T, X * LN), bf16),
+        pltpu.VMEM((F, T, 2 * LN), bf16),
+        pltpu.SemaphoreType.DMA((10,)),
+        pltpu.SemaphoreType.DMA((10,)),
     ]
     return pl.pallas_call(
         functools.partial(kernel, R, F),
@@ -587,21 +614,21 @@
         x_weight,
         z_weight,
         bc_weight,
-        dt_weight,
+        dt_weight.T,
         dt_bias.reshape(1, -1),
         decay_rate.reshape(1, -1),
         conv_x_weight,
-        conv_x_bias.reshape(1, -1),
+        conv_x_bias,
         conv_bc_weight,
-        conv_bc_bias.reshape(1, -1),
-        norm_gain.reshape(1, -1),
-        out_weight,
+        conv_bc_bias,
+        norm_gain,
+        out_weight.T,
         conv_x_state,
         conv_bc_state,
         ssm_state,
         sink_x,
         sink_b,
-        page_x,
+        jnp.swapaxes(page_x, 1, 2),
         page_b,
         page_decay,
         slot_req,

time: 96.4 us -> 90.5 us (0.939)
  Pallas kernels: 85.3 us -> 66.8 us
  local copies, waits for them, and re-layouts: 9 us -> 21.6 us
    pallas_call x1, Pallas kernels: 85.3 us -> 66.8 us  [per_device(): pl.pallas_call(functools.partial(kernel, R, F), out_shape=(shape((1, T, 2...]
    unnamed x45 -> x54, local copies, waits for them, and re-layouts: 6.98 us -> 21.6 us
    reshape x3 -> x0, local copies, waits for them, and re-layouts: 2.02 us -> none  [the longest x1 0.68 us: per_device(): conv_x_bias.reshape(1, -1)]
where the time goes in v2:
time: 90.5 us; the launch traced here: 89.7 us
  Pallas kernels  66.8 us (74%)
  local copies, waits for them, and re-layouts  21.6 us (24%)
  between operations  1.33 us (1%)
    pallas_call x1, Pallas kernels, per_device(): pl.pallas_call(functools.partial(kernel, R, F), out_shape=(shape((1, T, 2...  66.8 us
    unnamed x54, local copies, waits for them, and re-layouts  21.6 us

profile of v2, /device:TPU:1, one launch (start us, length us, event | category | flops | bytes accessed | tf_op | source)
XLA Modules:
  0.0 89.7 jit_solution(10229740407227645308)
XLA Ops:
  1.3 0.0 copy-start
  1.3 1.4 %copy-done = bf16[10,256,320]{1,2,0:T(8,128)(2,1)S(1)} copy-done((bf16[10,256,320]{1,2,0:T(8,128)(2,1)S(1)}, bf16[10,256,320]{1,2,0:T(8,128)(2,1)}, u32[]{:S(2)}) %copy-start) | copy-done | bytes 1638424
  2.7 0.0 copy-start.1
  2.7 1.1 %copy-done.1 = bf16[10,256,128]{2,1,0:T(8,128)(2,1)S(1)} copy-done((bf16[10,256,128]{2,1,0:T(8,128)(2,1)S(1)}, bf16[10,256,128]{2,1,0:T(8,128)(2,1)}, u32[]{:S(2)}) %copy-start.1) | copy-done | bytes 655384
  3.8 0.0 copy-start.2
  3.8 0.9 %copy-done.2 = f32[1,5,64,128]{3,2,1,0:T(8,128)S(1)} copy-done((f32[1,5,64,128]{3,2,1,0:T(8,128)S(1)}, f32[1,5,64,128]{3,2,1,0:T(8,128)}, u32[]{:S(2)}) %copy-start.2) | copy-done | bytes 163864
  4.7 0.0 copy-start.3
  4.7 0.9 copy-done.3
  5.6 0.0 copy-start.4
  5.6 0.9 copy-done.4
  6.5 0.0 copy-start.5
  6.5 0.8 copy-done.5
  7.3 0.0 copy-start.6
  7.3 0.8 copy-done.6
  8.2 0.0 copy-start.7
  8.2 0.8 copy-done.7
  9.0 0.0 copy-start.8
  9.0 0.8 copy-done.8
  9.8 0.0 copy-start.9
  9.8 0.7 copy-done.9
  10.5 0.7 copy-done.10
  11.1 0.0 copy-start.11
  11.1 0.7 copy-done.11
  11.8 0.0 copy-start.12
  11.8 0.7 copy-done.12
  12.5 0.0 copy-start.13
  12.5 0.7 copy-done.13
  13.2 0.0 copy-start.14
  13.2 0.7 copy-done.14
  13.9 0.0 copy-start.15
  13.9 0.7 copy-done.15
  14.5 0.0 copy-start.16
  14.5 0.7 copy-done.16
  15.2 0.0 copy-start.17
  15.2 0.7 copy-done.17
  15.9 0.0 copy-start.18
  15.9 0.7 copy-done.18
  16.6 0.7 copy-done.19
  17.2 0.7 copy-done.20
  17.9 0.7 copy-done.21
  18.5 0.7 copy-done.22
  19.2 0.7 copy-done.23
  19.8 0.7 copy-done.24
  20.5 66.8 %mixer.1 = (bf16[1,16,160]{2,1,0:T(8,128)(2,1)S(1)}, f32[1,5,64,128]{3,2,1,0:T(8,128)S(1)}, bf16[1,3,320]{2,1,0:T(4,128)(2,1)S(1)}, bf16[1,3,256]{2,1,0:T(4,128)(2,1)S(1)}) custom-call(bf16[1,16,2560]{2,1,0:T(8,128)(2,1)S(1)} %copy-done.3, bf16[80,320]{1,0:T(8,128)(2,1)S(1)} %copy-done.5, bf16[80,320]{1,0:T(8,128)(2,1)S(1)} %copy-done.6, ...), custom_call_target="tpu_custom_call" | custom-call | tf_op jit(solution)/shard_map/mixer/pallas_call | solution.py:597
  87.3 0.6 copy.35
  87.9 0.7 copy.36
  88.6 0.6 copy.37
  89.1 0.6 copy.38
  (7 shorter events, 0.0 us)
Async XLA Ops:
  1.3 1.4 %copy-start = (bf16[10,256,320]{1,2,0:T(8,128)(2,1)S(1)}, bf16[10,256,320]{1,2,0:T(8,128)(2,1)}, u32[]{:S(2)}) copy-start(bf16[10,256,320]{1,2,0:T(8,128)(2,1)} %param.44) | copy-start | bytes 4915204
  2.7 1.1 %copy-start.1 = (bf16[10,256,128]{2,1,0:T(8,128)(2,1)S(1)}, bf16[10,256,128]{2,1,0:T(8,128)(2,1)}, u32[]{:S(2)}) copy-start(bf16[10,256,128]{2,1,0:T(8,128)(2,1)} %page_b_ref.1) | copy-start | bytes 1966084
  3.8 0.9 %copy-start.2 = (f32[1,5,64,128]{3,2,1,0:T(8,128)S(1)}, f32[1,5,64,128]{3,2,1,0:T(8,128)}, u32[]{:S(2)}) copy-start(f32[1,5,64,128]{3,2,1,0:T(8,128)} %ssm_ref.1) | copy-start | bytes 491524
  4.7 0.9 copy-start.3
  5.6 0.9 copy-start.4
  6.5 0.8 copy-start.5
  7.3 0.8 copy-start.6
  8.2 0.8 copy-start.7
  9.0 0.8 copy-start.8
  9.8 0.7 copy-start.9
  10.4 0.7 copy-start.10
  11.1 0.7 copy-start.11
  11.8 0.7 copy-start.12
  12.5 0.7 copy-start.13
  13.2 0.7 copy-start.14
  13.9 0.7 copy-start.15
  14.5 0.7 copy-start.16
  15.2 0.7 copy-start.17
  15.9 0.7 copy-start.18
  16.6 0.7 copy-start.19
  17.2 0.7 copy-start.20
  17.9 0.7 copy-start.21
  18.5 0.7 copy-start.22
  19.2 0.7 copy-start.23
  19.8 0.7 copy-start.24

commit v3 on v2

--- a/solution.py
+++ b/solution.py
@@ -9,6 +9,7 @@
 
 MESH = pl.DeviceIdType.MESH
 T = 16
+CROWS = 24
 X = 4
 KC = 4
 HD = 64
@@ -17,6 +18,38 @@
 f32 = jnp.float32
 bf16 = jnp.bfloat16
 EXACT = lax.Precision.HIGHEST
+NAMES = (
+    "drafts",
+    "xw",
+    "zw",
+    "bcw",
+    "dtw",
+    "dt_bias",
+    "decay",
+    "cxw",
+    "cxb",
+    "cbw",
+    "cbb",
+    "gain",
+    "ow",
+    "cxs",
+    "cbs",
+    "ssm",
+    "sink_x",
+    "sink_b",
+    "page_x",
+    "page_b",
+    "page_decay",
+    "slot_req",
+    "slot_page",
+    "page_count",
+    "accepted",
+    "owner_row",
+)
+SCALARS = ("slot_req", "slot_page", "page_count", "owner_row")
+FIRST = ("bcw", "dtw")
+SECOND = ("xw", "zw", "drafts", "ow", "page_decay", "page_x", "page_b")
+OTHERS = tuple(n for n in NAMES if n not in FIRST + SECOND)
 
 
 def nt(a, b, precision=None):
@@ -41,9 +74,30 @@
     return hi, mid, low
 
 
-def kernel(
+def kernel(R, F, *refs):
+    sources, outs, held, rest = refs[:26], refs[26:30], refs[30:56], refs[56:-1]
+    load_sem = refs[-1]
+    copies = [
+        pltpu.make_async_copy(source, target, load_sem.at[i])
+        for i, (source, target) in enumerate(zip(sources, held))
+    ]
+
+    def load(*names):
+        for name in names:
+            copies[NAMES.index(name)].start()
+
+    def arrive(*names):
+        for name in names:
+            copies[NAMES.index(name)].wait()
+
+    body(R, F, load, arrive, *held, *outs, *rest)
+
+
+def body(
     R,
     F,
+    load,
+    arrive,
     drafts_ref,
     xw_ref,
     zw_ref,
@@ -88,6 +142,8 @@
     s_bc,
     cc_own,
     cc_all,
+    state_buf,
+    least_buf,
     q_buf,
     cum_buf,
     w5,
@@ -121,6 +177,7 @@
     mx = lax.rem(me, X)
     is_self = lax.div(mf, per_row) == my
 
+    load(*FIRST)
     barrier = pltpu.get_barrier_semaphore()
 
     @pl.loop(1, R)
@@ -147,6 +204,9 @@
                 barrier, inc=1, device_id={"req": source, "fsdp": g}, device_id_type=MESH
             )
 
+    load(*SECOND)
+    load(*OTHERS)
+    arrive("bcw", "dtw")
     wpad = jnp.concatenate([bcw_ref[...], jnp.zeros((LN - ks, 2 * ns), bf16)], axis=0)
     pick = (iota((T, 2 * ns), 1) == T * mf + iota((T, 2 * ns), 0)).astype(bf16)
     bc_rows = nt(pick, wpad)
@@ -199,8 +259,10 @@
     tail = pad_in - inner
     for i in range(X):
         wxz[pl.ds(LN * i + ks, LN - ks), :] = jnp.zeros((LN - ks, 2 * inner), bf16)
+    arrive("xw", "zw")
     wxz[own_block, pl.ds(0, inner)] = xw_ref[...]
     wxz[own_block, pl.ds(inner, inner)] = zw_ref[...]
+    arrive("ow")
     w_ext[own_outs, pl.ds(0, inner)] = ow_ref[...]
     w_ext[own_outs, pl.ds(inner, tail)] = jnp.zeros((ocols, tail), bf16)
     rest = 2 * LN - 2 * ocols
@@ -216,6 +278,7 @@
         r = my * X + lax.rem(mx + i, X)
         put(wxz.at[own_block, :], wxz.at[own_block, :], 8, {"req": r})
 
+    arrive("drafts")
     a_buf[pl.ds(48, LN - 48), :] = jnp.zeros((LN - 48, R * LN), bf16)
     for j in range(R):
         start = ks * j
@@ -252,9 +315,10 @@
         r = my * X + lax.rem(mx + i, X)
         put(w_ext.at[own_outs, :], w_ext.at[own_outs, :], 9, {"req": r})
 
+    arrive("dt_bias", "decay", "cbs", "cxs", "sink_b", "sink_x")
     head_buf[...] = jnp.zeros(head_buf.shape, f32)
-    head_buf[pl.ds(0, 1), pl.ds(0, heads)] = dt_bias_ref[...]
-    head_buf[pl.ds(1, 1), pl.ds(0, heads)] = decay_ref[...]
+    head_buf[pl.ds(0, 1), pl.ds(0, heads)] = dt_bias_ref[...].reshape(1, heads)
+    head_buf[pl.ds(1, 1), pl.ds(0, heads)] = decay_ref[...].reshape(1, heads)
     s_bc[...] = jnp.zeros(s_bc.shape, f32)
     s_bc[pl.ds(T - KC + 1, KC - 1), :] = cbs_ref[0].astype(f32)
     s_x[...] = jnp.zeros(s_x.shape, f32)
@@ -263,6 +327,7 @@
     bs_buf[pl.ds(T, 4), :] = sink_b_ref[0].astype(f32)
     xs_buf[...] = jnp.zeros(xs_buf.shape, f32)
     xs_buf[pl.ds(T, 4), :] = sink_x_ref[0].astype(f32)
+    arrive("slot_req", "slot_page", "page_count", "owner_row", "accepted")
     rows_of = []
     live_of = []
     for s in range(slots):
@@ -276,17 +341,37 @@
     for s in range(slots):
         in_sub = lax.div(iota((slots * T, 1), 0), T) == s
         in_lane = lax.div(iota((1, slots * T), 1), T) == s
-        by_sub = jnp.where(in_sub, T * (rows_of[s] - s), by_sub)
+        by_sub = jnp.where(in_sub, rows_of[s], by_sub)
         live_sub = jnp.where(in_sub, live_of[s].astype(jnp.int32), live_sub)
         by_lane = jnp.where(
-            in_lane, jnp.where(live_of[s], T * (rows_of[s] - s), -(1 << 20)), by_lane
+            in_lane, jnp.where(live_of[s], rows_of[s], -(1 << 20)), by_lane
         )
-    gather_rows = (
-        iota((slots * T, R * T), 1) == iota((slots * T, R * T), 0) + by_sub
-    ).astype(bf16)
-    scatter_rows = (
-        iota((R * T, slots * T), 0) == iota((R * T, slots * T), 1) + by_lane
-    ).astype(bf16)
+    wide_lane = iota((slots * T, R * CROWS), 1)
+    at = lax.rem(iota((slots * T, 1), 0), T)
+    gather_c = (wide_lane == CROWS * by_sub + at).astype(bf16)
+    gather_cum = (wide_lane == CROWS * by_sub + T + lax.div(at, 8)).astype(bf16)
+    at = lax.rem(iota((1, slots * T), 1), T)
+    tall_sub = iota((R * 8, slots * T), 0)
+    scatter_low = ((tall_sub == 8 * by_lane + at) & (at < 8)).astype(bf16)
+    scatter_high = ((tall_sub == 8 * by_lane + at - 8) & (at >= 8)).astype(bf16)
+
+    arrive("cbb", "cbw", "cxb", "cxw", "gain", "ssm", "page_x", "page_b", "page_decay")
+
+    eye_h = iota((heads, LN), 0) == iota((heads, LN), 1)
+
+    @pl.loop(0, slots)
+    def _(s):
+        decays = page_decay_ref[s]
+        least = jnp.min(decays, axis=1, keepdims=True)
+        least_buf[s] = jnp.sum(jnp.where(eye_h, least, 0.0), axis=0, keepdims=True)
+        factor = jnp.exp(least - decays)
+        for h in range(heads):
+            rows = pl.ds(h * HD, HD)
+            faded = page_x_ref[s, rows, :].astype(f32) * factor[h : h + 1, :]
+            state_buf[s, rows, :] = jnp.dot(
+                faded.astype(bf16), page_b_ref[s], preferred_element_type=f32
+            ).astype(bf16)
+
 
     wait_bytes(w_all.at[:, pl.ds(0, (R - 1) * LN)], recv_sem.at[0])
     proj = nt(a_buf[...], w_all[...])
@@ -312,7 +397,14 @@
         upto, dtime * head_buf[pl.ds(1, 1), :], precision=EXACT, preferred_element_type=f32
     )
     hi, mid, low = pieces3(cumul)
-    packed = hi + pltpu.roll(mid, 16, 1) + pltpu.roll(low, 32, 1)
+    packed = hi + pltpu.roll(mid, 5, 1) + pltpu.roll(low, 10, 1)
+    for step in (16, 32, 64):
+        packed = packed + pltpu.roll(packed, step, 1)
+    packed = jnp.where(lax.div(el, T) == lax.rem(er, 8), packed, 0.0)
+    packed_low = jnp.sum(jnp.where(er < 8, packed, 0.0), axis=0, keepdims=True)
+    packed_high = jnp.sum(jnp.where(er >= 8, packed, 0.0), axis=0, keepdims=True)
+    row8 = iota((8, LN), 0)
+    packed = jnp.where(row8 == 0, packed_low, jnp.where(row8 == 1, packed_high, 0.0))
 
     wait_bytes(z_all.at[pl.ds(0, (F - 1) * T), :], recv_sem.at[2])
     bc_raw = nt((iota((T, LN), 0) == iota((T, LN), 1)).astype(bf16), z_all[...])
@@ -323,13 +415,15 @@
     bc_act = silu(acc)
     b_mat = bc_act[:, :ns].astype(bf16)
     c_mat = bc_act[:, ns:].astype(bf16)
-    cc_own[:, pl.ds(0, ns)] = c_mat
-    cc_own[:, pl.ds(ns, LN)] = packed.astype(bf16)
-    cc_all[own_rows, :] = cc_own[...]
+    if ns < LN:
+        cc_own[...] = jnp.zeros(cc_own.shape, bf16)
+    cc_own[pl.ds(0, T), pl.ds(0, ns)] = c_mat
+    cc_own[pl.ds(T, 8), :] = packed.astype(bf16)
+    cc_all[me] = cc_own[...]
 
     @pl.loop(1, R)
     def _(i):
-        put(cc_own, cc_all.at[own_rows, :], 3, {"req": lax.rem(me + i, R)})
+        put(cc_own, cc_all.at[me], 3, {"req": lax.rem(me + i, R)})
 
     wait_bytes(d_all.at[pl.ds(0, (Y - 1) * T), :], recv_sem.at[1])
     wait_bytes(w_bytes, recv_sem.at[8])
@@ -354,34 +448,37 @@
             out = jnp.where(head_lane == h, stacked[h * T : (h + 1) * T], out)
         return out
 
-    wait_bytes(cc_all.at[pl.ds(0, (R - 1) * T), :], recv_sem.at[3])
-    picked = jnp.dot(gather_rows, cc_all[...], preferred_element_type=f32)
-    q_buf[...] = picked[:, :ns].astype(bf16)
-    cum3 = picked[:, ns:]
-    cum_buf[...] = cum3 + pltpu.roll(cum3, LN - 16, 1) + pltpu.roll(cum3, LN - 32, 1)
-
-    @pl.loop(0, slots)
-    def _(s):
-        rows = pl.ds(pl.multiple_of(s * T, T), T)
-        scores = nt(q_buf[rows, :], page_b_ref[s])
-        cum = cum_buf[rows, :]
-        decays = page_decay_ref[s]
+    wait_bytes(cc_all.at[pl.ds(0, R - 1)], recv_sem.at[3])
+    cc = cc_all[...].reshape(R * CROWS, LN)
+    q_buf[...] = jnp.dot(gather_c, cc, preferred_element_type=f32)[:, :ns].astype(bf16)
+    cum3 = jnp.dot(gather_cum, cc, preferred_element_type=f32)
+    at = lax.rem(iota((slots * T, LN), 0), T)
+    el = iota((slots * T, LN), 1)
+    cum3 = jnp.where(lax.div(el, T) == lax.rem(at, 8), cum3, 0.0)
+    for step in (64, 32, 16):
+        cum3 = cum3 + pltpu.roll(cum3, step, 1)
+    cum = cum3 + pltpu.roll(cum3, LN - 5, 1) + pltpu.roll(cum3, LN - 10, 1)
+    cum_buf[...] = cum
+
+    for s in range(slots):
+        rows = pl.ds(s * T, T)
+        factor = jnp.exp(cum_buf[rows, :] - least_buf[s])
+        spread = jnp.zeros((T, inner), f32)
         for h in range(heads):
-            factor = jnp.exp(cum[:, h : h + 1] - decays[h : h + 1, :])
-            w5[pl.ds(h * T, T), :] = (scores * factor).astype(bf16)
-        stacked = nt(w5[...], page_x_ref[s])
-        terms[rows, :] = own_heads(stacked)
+            spread = jnp.where(head_lane == h, factor[:, h : h + 1], spread)
+        terms[rows, :] = nt(q_buf[rows, :], state_buf[s]) * spread
 
     kept_terms = jnp.where(live_sub != 0, terms[...], 0.0).astype(bf16)
-    summed = jnp.dot(scatter_rows, kept_terms, preferred_element_type=f32)
-    p_send[:, pl.ds(0, inner)] = summed.astype(bf16)
-    p_send[:, pl.ds(inner, tail)] = jnp.zeros((R * T, tail), bf16)
-    p_recv[me] = p_send[own_rows, :]
+    low = jnp.dot(scatter_low, kept_terms, preferred_element_type=f32)
+    high = jnp.dot(scatter_high, kept_terms, preferred_element_type=f32)
+    p_send[:, :, pl.ds(0, inner)] = low.astype(bf16).reshape(R, 8, inner)
+    p_send[:, :, pl.ds(inner, inner)] = high.astype(bf16).reshape(R, 8, inner)
+    p_recv[me] = p_send[me]
 
     @pl.loop(1, R)
     def _(i):
         r = lax.rem(me + i, R)
-        put(p_send.at[pl.ds(pl.multiple_of(r * T, T), T), :], p_recv.at[me], 5, {"req": r})
+        put(p_send.at[r], p_recv.at[me], 5, {"req": r})
 
     wait_bytes(xz_recv.at[pl.ds(0, Y - 1)], recv_sem.at[4])
     xz = lax.fori_loop(
@@ -414,7 +511,7 @@
         )
     )
 
-    taken = accepted_ref[0]
+    taken = accepted_ref[...]
     at = iota((T, LN), 0)
     last = jnp.sum(jnp.where(at == taken - 1, cumul, 0.0), axis=0, keepdims=True)
     spread = jnp.where(at < taken, last - cumul, 0.0)
@@ -444,7 +541,8 @@
     wait_bytes(p_recv.at[pl.ds(0, R - 1)], recv_sem.at[5])
     page_sum = lax.fori_loop(
         1, R, lambda i, total: total + p_recv[i].astype(f32), p_recv[0].astype(f32)
-    )[:, :inner]
+    )
+    page_sum = jnp.concatenate([page_sum[:, :inner], page_sum[:, inner:]], axis=0)
     gated = (page_sum + local) * gate
     squares = jnp.sum(gated * gated, axis=1, keepdims=True)
     hi, mid, low = pieces3(squares)
@@ -506,7 +604,7 @@
     wait_bytes(w_all.at[:, pl.ds(0, (R - 1) * LN)], send_sem.at[0])
     wait_bytes(d_all.at[pl.ds(0, (Y - 1) * T), :], send_sem.at[1])
     wait_bytes(z_all.at[pl.ds(0, (F - 1) * T), :], send_sem.at[2])
-    wait_bytes(cc_all.at[pl.ds(0, (R - 1) * T), :], send_sem.at[3])
+    wait_bytes(cc_all.at[pl.ds(0, R - 1)], send_sem.at[3])
     wait_bytes(xz_recv.at[pl.ds(0, Y - 1)], send_sem.at[4])
     wait_bytes(w_bytes, send_sem.at[8])
     wait_bytes(o_bytes, send_sem.at[9])
@@ -520,6 +618,15 @@
     @pl.when(jnp.logical_not(is_self))
     def _():
         wait_bytes(f_recv, send_sem.at[7])
+
+
+def hand_over(*refs):
+    sem = refs[8]
+    copies = [pltpu.make_async_copy(refs[i], refs[4 + i], sem.at[i]) for i in range(4)]
+    for copy in copies:
+        copy.start()
+    for copy in copies:
+        copy.wait()
 
 
 def per_device(
@@ -560,63 +667,15 @@
     pad_in = -(-inner // LN) * LN
     Y = R // X
     vmem = pl.BlockSpec(memory_space=pltpu.VMEM)
-    smem = pl.BlockSpec(memory_space=pltpu.SMEM)
     shape = jax.ShapeDtypeStruct
-    scratch = [
-        pltpu.VMEM((T, LN), f32),
-        pltpu.VMEM((LN, R * LN), bf16),
-        pltpu.VMEM((T, LN), bf16),
-        pltpu.VMEM((T, R * LN), bf16),
-        pltpu.VMEM((Y * T, X * LN), bf16),
-        pltpu.VMEM((X * LN, 2 * inner), bf16),
-        pltpu.VMEM((Y * T, 2 * inner), bf16),
-        pltpu.VMEM((Y, T, 2 * inner), bf16),
-        pltpu.VMEM((T, LN), bf16),
-        pltpu.VMEM((F * T, LN), bf16),
-        pltpu.VMEM((8, LN), f32),
-        pltpu.VMEM((2 * T, 2 * ns), f32),
-        pltpu.VMEM((T, ns + LN), bf16),
-        pltpu.VMEM((R * T, ns + LN), bf16),
-        pltpu.VMEM((slots * T, ns), bf16),
-        pltpu.VMEM((slots * T, LN), f32),
-        pltpu.VMEM((heads * T, page), bf16),
-        pltpu.VMEM((slots * T, inner), f32),
-        pltpu.VMEM((R * T, pad_in), bf16),
-        pltpu.VMEM((R, T, pad_in), bf16),
-        pltpu.VMEM((2 * T, inner), f32),
-        pltpu.VMEM((2 * T, inner), f32),
-        pltpu.VMEM((2 * T, ns), f32),
-        pltpu.VMEM((T, pad_in), bf16),
-        pltpu.VMEM((Y * T, pad_in), bf16),
-        pltpu.VMEM((X * LN, pad_in), bf16),
-        pltpu.VMEM((Y * T, X * LN), bf16),
-        pltpu.VMEM((F, T, 2 * LN), bf16),
-        pltpu.SemaphoreType.DMA((10,)),
-        pltpu.SemaphoreType.DMA((10,)),
-    ]
-    return pl.pallas_call(
-        functools.partial(kernel, R, F),
-        out_shape=(
-            shape((1, T, 2 * ocols), bf16),
-            shape(ssm_state.shape, f32),
-            shape(conv_x_state.shape, bf16),
-            shape(conv_bc_state.shape, bf16),
-        ),
-        in_specs=[vmem] * 21 + [smem] * 5,
-        out_specs=(vmem,) * 4,
-        scratch_shapes=scratch,
-        compiler_params=pltpu.CompilerParams(
-            collective_id=0, has_side_effects=True, vmem_limit_bytes=48 << 20
-        ),
-        name="mixer",
-    )(
+    operands = (
         drafts,
         x_weight,
         z_weight,
         bc_weight,
         dt_weight.T,
-        dt_bias.reshape(1, -1),
-        decay_rate.reshape(1, -1),
+        dt_bias,
+        decay_rate,
         conv_x_weight,
         conv_x_bias,
         conv_bc_weight,
@@ -634,9 +693,73 @@
         slot_req,
         slot_page,
         page_count,
-        accepted,
+        accepted.reshape(1, 1),
         owner_row,
     )
+    held = [
+        (pltpu.SMEM if name in SCALARS else pltpu.VMEM)(a.shape, a.dtype)
+        for name, a in zip(NAMES, operands)
+    ]
+    scratch = held + [
+        pltpu.VMEM((T, LN), f32),
+        pltpu.VMEM((LN, R * LN), bf16),
+        pltpu.VMEM((T, LN), bf16),
+        pltpu.VMEM((T, R * LN), bf16),
+        pltpu.VMEM((Y * T, X * LN), bf16),
+        pltpu.VMEM((X * LN, 2 * inner), bf16),
+        pltpu.VMEM((Y * T, 2 * inner), bf16),
+        pltpu.VMEM((Y, T, 2 * inner), bf16),
+        pltpu.VMEM((T, LN), bf16),
+        pltpu.VMEM((F * T, LN), bf16),
+        pltpu.VMEM((8, LN), f32),
+        pltpu.VMEM((2 * T, 2 * ns), f32),
+        pltpu.VMEM((CROWS, LN), bf16),
+        pltpu.VMEM((R, CROWS, LN), bf16),
+        pltpu.VMEM((slots, inner, ns), bf16),
+        pltpu.VMEM((slots, 1, LN), f32),
+        pltpu.VMEM((slots * T, ns), bf16),
+        pltpu.VMEM((slots * T, LN), f32),
+        pltpu.VMEM((heads * T, page), bf16),
+        pltpu.VMEM((slots * T, inner), f32),
+        pltpu.VMEM((R, 8, 2 * inner), bf16),
+        pltpu.VMEM((R, 8, 2 * inner), bf16),
+        pltpu.VMEM((2 * T, inner), f32),
+        pltpu.VMEM((2 * T, inner), f32),
+        pltpu.VMEM((2 * T, ns), f32),
+        pltpu.VMEM((T, pad_in), bf16),
+        pltpu.VMEM((Y * T, pad_in), bf16),
+        pltpu.VMEM((X * LN, pad_in), bf16),
+        pltpu.VMEM((Y * T, X * LN), bf16),
+        pltpu.VMEM((F, T, 2 * LN), bf16),
+        pltpu.SemaphoreType.DMA((10,)),
+        pltpu.SemaphoreType.DMA((10,)),
+        pltpu.SemaphoreType.DMA((26,)),
+    ]
+    results = pl.pallas_call(
+        functools.partial(kernel, R, F),
+        out_shape=(
+            shape((1, T, 2 * ocols), bf16),
+            shape(ssm_state.shape, f32),
+            shape(conv_x_state.shape, bf16),
+            shape(conv_bc_state.shape, bf16),
+        ),
+        in_specs=[pl.BlockSpec(memory_space=pltpu.HBM)] * 26,
+        out_specs=(vmem,) * 4,
+        scratch_shapes=scratch,
+        compiler_params=pltpu.CompilerParams(
+            collective_id=0, has_side_effects=True
+        ),
+        name="mixer",
+    )(*operands)
+    hbm = pl.BlockSpec(memory_space=pltpu.HBM)
+    return pl.pallas_call(
+        hand_over,
+        out_shape=tuple(shape(a.shape, a.dtype) for a in results),
+        in_specs=[hbm] * 4,
+        out_specs=(hbm,) * 4,
+        scratch_shapes=[pltpu.SemaphoreType.DMA((4,))],
+        name="hand_over",
+    )(*results)
 
 
 def solution(mesh):

time: 90.5 us -> 70.9 us (0.78)
  local copies, waits for them, and re-layouts: 21.6 us -> 0 us
  Pallas kernels: 66.8 us -> 69.4 us
    unnamed x54 -> x0, local copies, waits for them, and re-layouts: 21.6 us -> none
    pallas_call x0 -> x1, Pallas kernels: none -> 6.51 us  [per_device(): pl.pallas_call(hand_over, out_shape=tuple((shape(a.shape, a.dtype) for a...]
    pallas_call x1, Pallas kernels: 66.8 us -> 62.9 us  [per_device(): pl.pallas_call(functools.partial(kernel, R, F), out_shape=(shape((1, T, 2...]
where the time goes in v3:
time: 70.9 us; the launch traced here: 70.7 us
  Pallas kernels  69.4 us (98%)
  between operations  1.3 us (2%)
    pallas_call x1, Pallas kernels, per_device(): pl.pallas_call(functools.partial(kernel, R, F), out_shape=(shape((1, T, 2...  62.9 us
    pallas_call x1, Pallas kernels, per_device(): pl.pallas_call(hand_over, out_shape=tuple((shape(a.shape, a.dtype) for a...  6.51 us

profile of v3, /device:TPU:1, one launch (start us, length us, event | category | flops | bytes accessed | tf_op | source)
XLA Modules:
  0.0 70.7 jit_solution(18101104872604388844)
XLA Ops:
  1.3 62.9 %mixer.1 = (bf16[1,16,160]{2,1,0:T(8,128)(2,1)}, f32[1,5,64,128]{3,2,1,0:T(8,128)}, bf16[1,3,320]{2,1,0:T(4,128)(2,1)}, bf16[1,3,256]{2,1,0:T(4,128)(2,1)}) custom-call(bf16[1,16,2560]{2,1,0:T(8,128)(2,1)} %refs_0_.1, bf16[80,320]{1,0:T(8,128)(2,1)} %refs_1_.1, bf16[80,320]{1,0:T(8,128)(2,1)} %refs_2_.1, bf16[80,256]{1,0:T(8,128)(2,1)} %refs_3_.1, ...), custom_call_target="tpu_custom_call" | custom-call | tf_op jit(solution)/shard_map/mixer/pallas_call | solution.py:738
  64.2 6.5 %hand_over.1 = (bf16[1,16,160]{2,1,0:T(8,128)(2,1)}, f32[1,5,64,128]{3,2,1,0:T(8,128)}, bf16[1,3,320]{2,1,0:T(4,128)(2,1)}, bf16[1,3,256]{2,1,0:T(4,128)(2,1)}) custom-call(bf16[1,16,160]{2,1,0:T(8,128)(2,1)} %get-tuple-element.8.refs_0_, f32[1,5,64,128]{3,2,1,0:T(8,128)} %get-tuple-element.9.refs_1_, bf16[1,3,320]{2,1,0:T(4,128)(2,1)} %get-tuple-element.10.refs_2_, ...), custom_call_target="tpu_custom_call" | custom-call | tf_op jit(solution)/shard_map/hand_over/pallas_call | solution.py:755

commit v4 on v3

--- a/solution.py
+++ b/solution.py
@@ -48,7 +48,7 @@
 )
 SCALARS = ("slot_req", "slot_page", "page_count", "owner_row")
 FIRST = ("bcw", "dtw")
-SECOND = ("xw", "zw", "drafts", "ow", "page_decay", "page_x", "page_b")
+SECOND = ("drafts", "xw", "zw", "ow")
 OTHERS = tuple(n for n in NAMES if n not in FIRST + SECOND)
 
 
@@ -75,8 +75,12 @@
 
 
 def kernel(R, F, *refs):
-    sources, outs, held, rest = refs[:26], refs[26:30], refs[30:56], refs[56:-1]
-    load_sem = refs[-1]
+    sources, outs, held, rest = refs[:26], refs[26:30], refs[30:56], refs[56:-6]
+    ready, load_sem, store_sem = refs[-6:-2], refs[-2], refs[-1]
+    stores = [
+        pltpu.make_async_copy(source, target, store_sem.at[i])
+        for i, (source, target) in enumerate(zip(ready, outs))
+    ]
     copies = [
         pltpu.make_async_copy(source, target, load_sem.at[i])
         for i, (source, target) in enumerate(zip(sources, held))
@@ -90,7 +94,9 @@
         for name in names:
             copies[NAMES.index(name)].wait()
 
-    body(R, F, load, arrive, *held, *outs, *rest)
+    body(R, F, load, arrive, stores, *held, *ready, *rest)
+    for store in stores:
+        store.wait()
 
 
 def body(
@@ -98,6 +104,7 @@
     F,
     load,
     arrive,
+    stores,
     drafts_ref,
     xw_ref,
     zw_ref,
@@ -147,9 +154,10 @@
     q_buf,
     cum_buf,
     w5,
-    terms,
-    p_send,
-    p_recv,
+    pa_send,
+    pa_recv,
+    pb_send,
+    pb_recv,
     s_x,
     xs_buf,
     bs_buf,
@@ -205,7 +213,6 @@
             )
 
     load(*SECOND)
-    load(*OTHERS)
     arrive("bcw", "dtw")
     wpad = jnp.concatenate([bcw_ref[...], jnp.zeros((LN - ks, 2 * ns), bf16)], axis=0)
     pick = (iota((T, 2 * ns), 1) == T * mf + iota((T, 2 * ns), 0)).astype(bf16)
@@ -251,6 +258,8 @@
     @pl.loop(1, R)
     def _(i):
         put(w_own, w_all.at[:, own_lanes], 0, {"req": lax.rem(me + i, R)})
+
+    load(*OTHERS)
 
     own_block = pl.ds(pl.multiple_of(mx * LN, LN), ks)
     own_outs = pl.ds(
@@ -279,7 +288,7 @@
         put(wxz.at[own_block, :], wxz.at[own_block, :], 8, {"req": r})
 
     arrive("drafts")
-    a_buf[pl.ds(48, LN - 48), :] = jnp.zeros((LN - 48, R * LN), bf16)
+    z_own[...] = jnp.zeros(z_own.shape, bf16)
     for j in range(R):
         start = ks * j
         base = start // LN * LN
@@ -327,6 +336,91 @@
     bs_buf[pl.ds(T, 4), :] = sink_b_ref[0].astype(f32)
     xs_buf[...] = jnp.zeros(xs_buf.shape, f32)
     xs_buf[pl.ds(T, 4), :] = sink_x_ref[0].astype(f32)
+    arrive("cbb", "cbw", "cxb", "cxw", "gain", "ssm", "page_x", "page_b", "page_decay")
+
+    wait_bytes(w_all.at[:, pl.ds(0, (R - 1) * LN)], recv_sem.at[0])
+    proj = nt(a_buf[pl.ds(0, 3 * T), :], w_all[...])
+    z_own[:, pl.ds(0, 3 * T)] = nt((iota((T, T), 0) == iota((T, T), 1)).astype(bf16), proj.astype(bf16)).astype(bf16)
+    z_rows = pl.ds(pl.multiple_of(mf * T, T), T)
+    z_all[z_rows, :] = z_own[...]
+
+    @pl.loop(1, F)
+    def _(i):
+        put(z_own, z_all.at[z_rows, :], 2, {"fsdp": lax.rem(mf + i, F)})
+
+    wait_bytes(d_all.at[pl.ds(0, (Y - 1) * T), :], recv_sem.at[1])
+    wait_bytes(w_bytes, recv_sem.at[8])
+    xz_send[...] = jnp.dot(d_all[...], wxz[...], preferred_element_type=f32).astype(bf16)
+    xz_recv[my] = xz_send[y_rows, :]
+
+    @pl.loop(1, Y)
+    def _(i):
+        yy = lax.rem(my + i, Y)
+        put(
+            xz_send.at[pl.ds(pl.multiple_of(yy * T, T), T), :],
+            xz_recv.at[my],
+            4,
+            {"req": yy * X + mx},
+        )
+
+    er = iota((T, LN), 0)
+    el = iota((T, LN), 1)
+    first = ((er == el) & (el < heads)).astype(f32)
+    second = ((er == el + heads) & (el < heads)).astype(f32)
+    dt_raw = jnp.dot(proj[T : 2 * T], first, precision=EXACT, preferred_element_type=f32) + jnp.dot(
+        proj[2 * T : 3 * T], second, precision=EXACT, preferred_element_type=f32
+    )
+    v = dt_raw + head_buf[pl.ds(0, 1), :]
+    dtime = jnp.maximum(v, 0.0) + jnp.log1p(jnp.exp(-jnp.abs(v)))
+    upto = (iota((T, T), 1) <= iota((T, T), 0)).astype(f32)
+    cumul = -jnp.dot(
+        upto, dtime * head_buf[pl.ds(1, 1), :], precision=EXACT, preferred_element_type=f32
+    )
+    hi, mid, low = pieces3(cumul)
+    packed = hi + pltpu.roll(mid, 5, 1) + pltpu.roll(low, 10, 1)
+    for step in (16, 32, 64):
+        packed = packed + pltpu.roll(packed, step, 1)
+    packed = jnp.where(lax.div(el, T) == lax.rem(er, 8), packed, 0.0)
+    packed_low = jnp.sum(jnp.where(er < 8, packed, 0.0), axis=0, keepdims=True)
+    packed_high = jnp.sum(jnp.where(er >= 8, packed, 0.0), axis=0, keepdims=True)
+    row8 = iota((8, LN), 0)
+    packed = jnp.where(row8 == 0, packed_low, jnp.where(row8 == 1, packed_high, 0.0))
+
+    wait_bytes(z_all.at[pl.ds(0, (F - 1) * T), :], recv_sem.at[2])
+    bc_raw = nt((iota((T, LN), 0) == iota((T, LN), 1)).astype(bf16), z_all[...])
+    s_bc[pl.ds(T, T), :] = bc_raw
+    acc = jnp.zeros((T, 2 * ns), f32) + cbb_ref[...].astype(f32).reshape(1, 2 * ns)
+    for k in range(KC):
+        acc = acc + cbw_ref[pl.ds(k, 1), :].astype(f32) * s_bc[pl.ds(T - KC + 1 + k, T), :]
+    bc_act = silu(acc)
+    b_mat = bc_act[:, :ns].astype(bf16)
+    c_mat = bc_act[:, ns:].astype(bf16)
+    if ns < LN:
+        cc_own[...] = jnp.zeros(cc_own.shape, bf16)
+    cc_own[pl.ds(0, T), pl.ds(0, ns)] = c_mat
+    cc_own[pl.ds(T, 8), :] = packed.astype(bf16)
+    cc_all[me] = cc_own[...]
+
+    @pl.loop(1, R)
+    def _(i):
+        put(cc_own, cc_all.at[me], 3, {"req": lax.rem(me + i, R)})
+
+    eye_h = iota((heads, LN), 0) == iota((heads, LN), 1)
+
+    @pl.loop(0, slots)
+    def _(s):
+        decays = page_decay_ref[s]
+        least = jnp.min(decays, axis=1, keepdims=True)
+        least_buf[s] = jnp.sum(jnp.where(eye_h, least, 0.0), axis=0, keepdims=True)
+        factor = jnp.exp(least - decays)
+        for h in range(heads):
+            rows = pl.ds(h * HD, HD)
+            faded = page_x_ref[s, rows, :].astype(f32) * factor[h : h + 1, :]
+            state_buf[s, rows, :] = jnp.dot(
+                faded.astype(bf16), page_b_ref[s], preferred_element_type=f32
+            ).astype(bf16)
+
+
     arrive("slot_req", "slot_page", "page_count", "owner_row", "accepted")
     rows_of = []
     live_of = []
@@ -355,91 +449,6 @@
     scatter_low = ((tall_sub == 8 * by_lane + at) & (at < 8)).astype(bf16)
     scatter_high = ((tall_sub == 8 * by_lane + at - 8) & (at >= 8)).astype(bf16)
 
-    arrive("cbb", "cbw", "cxb", "cxw", "gain", "ssm", "page_x", "page_b", "page_decay")
-
-    eye_h = iota((heads, LN), 0) == iota((heads, LN), 1)
-
-    @pl.loop(0, slots)
-    def _(s):
-        decays = page_decay_ref[s]
-        least = jnp.min(decays, axis=1, keepdims=True)
-        least_buf[s] = jnp.sum(jnp.where(eye_h, least, 0.0), axis=0, keepdims=True)
-        factor = jnp.exp(least - decays)
-        for h in range(heads):
-            rows = pl.ds(h * HD, HD)
-            faded = page_x_ref[s, rows, :].astype(f32) * factor[h : h + 1, :]
-            state_buf[s, rows, :] = jnp.dot(
-                faded.astype(bf16), page_b_ref[s], preferred_element_type=f32
-            ).astype(bf16)
-
-
-    wait_bytes(w_all.at[:, pl.ds(0, (R - 1) * LN)], recv_sem.at[0])
-    proj = nt(a_buf[...], w_all[...])
-    z_own[...] = nt((iota((T, T), 0) == iota((T, T), 1)).astype(bf16), proj.astype(bf16)).astype(bf16)
-    z_rows = pl.ds(pl.multiple_of(mf * T, T), T)
-    z_all[z_rows, :] = z_own[...]
-
-    @pl.loop(1, F)
-    def _(i):
-        put(z_own, z_all.at[z_rows, :], 2, {"fsdp": lax.rem(mf + i, F)})
-
-    er = iota((T, LN), 0)
-    el = iota((T, LN), 1)
-    first = ((er == el) & (el < heads)).astype(f32)
-    second = ((er == el + heads) & (el < heads)).astype(f32)
-    dt_raw = jnp.dot(proj[T : 2 * T], first, precision=EXACT, preferred_element_type=f32) + jnp.dot(
-        proj[2 * T : 3 * T], second, precision=EXACT, preferred_element_type=f32
-    )
-    v = dt_raw + head_buf[pl.ds(0, 1), :]
-    dtime = jnp.maximum(v, 0.0) + jnp.log1p(jnp.exp(-jnp.abs(v)))
-    upto = (iota((T, T), 1) <= iota((T, T), 0)).astype(f32)
-    cumul = -jnp.dot(
-        upto, dtime * head_buf[pl.ds(1, 1), :], precision=EXACT, preferred_element_type=f32
-    )
-    hi, mid, low = pieces3(cumul)
-    packed = hi + pltpu.roll(mid, 5, 1) + pltpu.roll(low, 10, 1)
-    for step in (16, 32, 64):
-        packed = packed + pltpu.roll(packed, step, 1)
-    packed = jnp.where(lax.div(el, T) == lax.rem(er, 8), packed, 0.0)
-    packed_low = jnp.sum(jnp.where(er < 8, packed, 0.0), axis=0, keepdims=True)
-    packed_high = jnp.sum(jnp.where(er >= 8, packed, 0.0), axis=0, keepdims=True)
-    row8 = iota((8, LN), 0)
-    packed = jnp.where(row8 == 0, packed_low, jnp.where(row8 == 1, packed_high, 0.0))
-
-    wait_bytes(z_all.at[pl.ds(0, (F - 1) * T), :], recv_sem.at[2])
-    bc_raw = nt((iota((T, LN), 0) == iota((T, LN), 1)).astype(bf16), z_all[...])
-    s_bc[pl.ds(T, T), :] = bc_raw
-    acc = jnp.zeros((T, 2 * ns), f32) + cbb_ref[...].astype(f32).reshape(1, 2 * ns)
-    for k in range(KC):
-        acc = acc + cbw_ref[pl.ds(k, 1), :].astype(f32) * s_bc[pl.ds(T - KC + 1 + k, T), :]
-    bc_act = silu(acc)
-    b_mat = bc_act[:, :ns].astype(bf16)
-    c_mat = bc_act[:, ns:].astype(bf16)
-    if ns < LN:
-        cc_own[...] = jnp.zeros(cc_own.shape, bf16)
-    cc_own[pl.ds(0, T), pl.ds(0, ns)] = c_mat
-    cc_own[pl.ds(T, 8), :] = packed.astype(bf16)
-    cc_all[me] = cc_own[...]
-
-    @pl.loop(1, R)
-    def _(i):
-        put(cc_own, cc_all.at[me], 3, {"req": lax.rem(me + i, R)})
-
-    wait_bytes(d_all.at[pl.ds(0, (Y - 1) * T), :], recv_sem.at[1])
-    wait_bytes(w_bytes, recv_sem.at[8])
-    xz_send[...] = jnp.dot(d_all[...], wxz[...], preferred_element_type=f32).astype(bf16)
-    xz_recv[my] = xz_send[y_rows, :]
-
-    @pl.loop(1, Y)
-    def _(i):
-        yy = lax.rem(my + i, Y)
-        put(
-            xz_send.at[pl.ds(pl.multiple_of(yy * T, T), T), :],
-            xz_recv.at[my],
-            4,
-            {"req": yy * X + mx},
-        )
-
     head_lane = lax.div(iota((T, inner), 1), HD)
 
     def own_heads(stacked):
@@ -460,25 +469,30 @@
     cum = cum3 + pltpu.roll(cum3, LN - 5, 1) + pltpu.roll(cum3, LN - 10, 1)
     cum_buf[...] = cum
 
-    for s in range(slots):
-        rows = pl.ds(s * T, T)
-        factor = jnp.exp(cum_buf[rows, :] - least_buf[s])
-        spread = jnp.zeros((T, inner), f32)
-        for h in range(heads):
-            spread = jnp.where(head_lane == h, factor[:, h : h + 1], spread)
-        terms[rows, :] = nt(q_buf[rows, :], state_buf[s]) * spread
-
-    kept_terms = jnp.where(live_sub != 0, terms[...], 0.0).astype(bf16)
-    low = jnp.dot(scatter_low, kept_terms, preferred_element_type=f32)
-    high = jnp.dot(scatter_high, kept_terms, preferred_element_type=f32)
-    p_send[:, :, pl.ds(0, inner)] = low.astype(bf16).reshape(R, 8, inner)
-    p_send[:, :, pl.ds(inner, inner)] = high.astype(bf16).reshape(R, 8, inner)
-    p_recv[me] = p_send[me]
-
-    @pl.loop(1, R)
-    def _(i):
-        r = lax.rem(me + i, R)
-        put(p_send.at[r], p_recv.at[me], 5, {"req": r})
+    cut = 2 * HD
+    for first_head, send, recv, phase in ((0, pa_send, pa_recv, 5), (2, pb_send, pb_recv, 10)):
+        lanes = cut if first_head == 0 else inner - cut
+        part = pl.ds(first_head * HD, lanes)
+        lane_head = lax.div(iota((T, lanes), 1), HD) + first_head
+        chosen = []
+        for s in range(slots):
+            rows = pl.ds(s * T, T)
+            factor = jnp.exp(cum_buf[rows, :] - least_buf[s])
+            spread = jnp.zeros((T, lanes), f32)
+            for h in range(first_head, first_head + lanes // HD):
+                spread = jnp.where(lane_head == h, factor[:, h : h + 1], spread)
+            chosen.append(nt(q_buf[rows, :], state_buf[s, part, :]) * spread)
+        kept = jnp.where(live_sub != 0, jnp.concatenate(chosen, axis=0), 0.0).astype(bf16)
+        low = jnp.dot(scatter_low, kept, preferred_element_type=f32)
+        high = jnp.dot(scatter_high, kept, preferred_element_type=f32)
+        send[:, :, pl.ds(0, lanes)] = low.astype(bf16).reshape(R, 8, lanes)
+        send[:, :, pl.ds(lanes, lanes)] = high.astype(bf16).reshape(R, 8, lanes)
+        recv[me] = send[me]
+
+        @pl.loop(1, R)
+        def _(i, send=send, recv=recv, phase=phase):
+            r = lax.rem(me + i, R)
+            put(send.at[r], recv.at[me], phase, {"req": r})
 
     wait_bytes(xz_recv.at[pl.ds(0, Y - 1)], recv_sem.at[4])
     xz = lax.fori_loop(
@@ -536,13 +550,19 @@
     ncx_ref[0] = ncx[: KC - 1].astype(bf16)
     ncb = jnp.dot(tail_pick, s_bc[...].astype(bf16), preferred_element_type=f32)
     ncb_ref[0] = ncb[: KC - 1].astype(bf16)
+    for store in stores[1:]:
+        store.start()
     gate = silu(z_raw)
 
-    wait_bytes(p_recv.at[pl.ds(0, R - 1)], recv_sem.at[5])
-    page_sum = lax.fori_loop(
-        1, R, lambda i, total: total + p_recv[i].astype(f32), p_recv[0].astype(f32)
-    )
-    page_sum = jnp.concatenate([page_sum[:, :inner], page_sum[:, inner:]], axis=0)
+    parts = []
+    for recv, phase in ((pa_recv, 5), (pb_recv, 10)):
+        wait_bytes(recv.at[pl.ds(0, R - 1)], recv_sem.at[phase])
+        part = lax.fori_loop(
+            1, R, lambda i, total, recv=recv: total + recv[i].astype(f32), recv[0].astype(f32)
+        )
+        lanes = part.shape[1] // 2
+        parts.append(jnp.concatenate([part[:, :lanes], part[:, lanes:]], axis=0))
+    page_sum = jnp.concatenate(parts, axis=1)
     gated = (page_sum + local) * gate
     squares = jnp.sum(gated * gated, axis=1, keepdims=True)
     hi, mid, low = pieces3(squares)
@@ -600,6 +620,7 @@
     )
     scale = lax.rsqrt(total_squares / total_inner + EPSILON)
     mixed_ref[0] = (out * scale)[:, :wide].astype(bf16)
+    stores[0].start()
 
     wait_bytes(w_all.at[:, pl.ds(0, (R - 1) * LN)], send_sem.at[0])
     wait_bytes(d_all.at[pl.ds(0, (Y - 1) * T), :], send_sem.at[1])
@@ -608,7 +629,8 @@
     wait_bytes(xz_recv.at[pl.ds(0, Y - 1)], send_sem.at[4])
     wait_bytes(w_bytes, send_sem.at[8])
     wait_bytes(o_bytes, send_sem.at[9])
-    wait_bytes(p_recv.at[pl.ds(0, R - 1)], send_sem.at[5])
+    wait_bytes(pa_recv.at[pl.ds(0, R - 1)], send_sem.at[5])
+    wait_bytes(pb_recv.at[pl.ds(0, R - 1)], send_sem.at[10])
     wait_bytes(g_all.at[pl.ds(0, (Y - 1) * T), :], send_sem.at[6])
 
     @pl.when(is_self)
@@ -621,12 +643,16 @@
 
 
 def hand_over(*refs):
-    sem = refs[8]
-    copies = [pltpu.make_async_copy(refs[i], refs[4 + i], sem.at[i]) for i in range(4)]
-    for copy in copies:
-        copy.start()
-    for copy in copies:
-        copy.wait()
+    held, sem = refs[8:12], refs[12]
+    reads = [pltpu.make_async_copy(refs[i], held[i], sem.at[i]) for i in range(4)]
+    writes = [pltpu.make_async_copy(held[i], refs[4 + i], sem.at[4 + i]) for i in range(4)]
+    for read in reads:
+        read.start()
+    for read, write in zip(reads, writes):
+        read.wait()
+        write.start()
+    for write in writes:
+        write.wait()
 
 
 def per_device(
@@ -666,7 +692,6 @@
     ocols = out_weight.shape[1]
     pad_in = -(-inner // LN) * LN
     Y = R // X
-    vmem = pl.BlockSpec(memory_space=pltpu.VMEM)
     shape = jax.ShapeDtypeStruct
     operands = (
         drafts,
@@ -696,13 +721,19 @@
         accepted.reshape(1, 1),
         owner_row,
     )
+    out_shapes = (
+        shape((1, T, 2 * ocols), bf16),
+        shape(ssm_state.shape, f32),
+        shape(conv_x_state.shape, bf16),
+        shape(conv_bc_state.shape, bf16),
+    )
     held = [
         (pltpu.SMEM if name in SCALARS else pltpu.VMEM)(a.shape, a.dtype)
         for name, a in zip(NAMES, operands)
     ]
     scratch = held + [
         pltpu.VMEM((T, LN), f32),
-        pltpu.VMEM((LN, R * LN), bf16),
+        pltpu.VMEM((3 * T, R * LN), bf16),
         pltpu.VMEM((T, LN), bf16),
         pltpu.VMEM((T, R * LN), bf16),
         pltpu.VMEM((Y * T, X * LN), bf16),
@@ -720,9 +751,10 @@
         pltpu.VMEM((slots * T, ns), bf16),
         pltpu.VMEM((slots * T, LN), f32),
         pltpu.VMEM((heads * T, page), bf16),
-        pltpu.VMEM((slots * T, inner), f32),
-        pltpu.VMEM((R, 8, 2 * inner), bf16),
-        pltpu.VMEM((R, 8, 2 * inner), bf16),
+        pltpu.VMEM((R, 8, 4 * HD), bf16),
+        pltpu.VMEM((R, 8, 4 * HD), bf16),
+        pltpu.VMEM((R, 8, 2 * inner - 4 * HD), bf16),
+        pltpu.VMEM((R, 8, 2 * inner - 4 * HD), bf16),
         pltpu.VMEM((2 * T, inner), f32),
         pltpu.VMEM((2 * T, inner), f32),
         pltpu.VMEM((2 * T, ns), f32),
@@ -731,20 +763,17 @@
         pltpu.VMEM((X * LN, pad_in), bf16),
         pltpu.VMEM((Y * T, X * LN), bf16),
         pltpu.VMEM((F, T, 2 * LN), bf16),
-        pltpu.SemaphoreType.DMA((10,)),
-        pltpu.SemaphoreType.DMA((10,)),
+        pltpu.SemaphoreType.DMA((11,)),
+        pltpu.SemaphoreType.DMA((11,)),
+        *(pltpu.VMEM(a.shape, a.dtype) for a in out_shapes),
         pltpu.SemaphoreType.DMA((26,)),
+        pltpu.SemaphoreType.DMA((4,)),
     ]
     results = pl.pallas_call(
         functools.partial(kernel, R, F),
-        out_shape=(
-            shape((1, T, 2 * ocols), bf16),
-            shape(ssm_state.shape, f32),
-            shape(conv_x_state.shape, bf16),
-            shape(conv_bc_state.shape, bf16),
-        ),
+        out_shape=out_shapes,
         in_specs=[pl.BlockSpec(memory_space=pltpu.HBM)] * 26,
-        out_specs=(vmem,) * 4,
+        out_specs=(pl.BlockSpec(memory_space=pltpu.HBM),) * 4,
         scratch_shapes=scratch,
         compiler_params=pltpu.CompilerParams(
             collective_id=0, has_side_effects=True
@@ -757,7 +786,8 @@
         out_shape=tuple(shape(a.shape, a.dtype) for a in results),
         in_specs=[hbm] * 4,
         out_specs=(hbm,) * 4,
-        scratch_shapes=[pltpu.SemaphoreType.DMA((4,))],
+        scratch_shapes=[pltpu.VMEM(a.shape, a.dtype) for a in results]
+        + [pltpu.SemaphoreType.DMA((8,))],
         name="hand_over",
     )(*results)
 

time: 70.9 us -> 65.1 us (0.918)
  Pallas kernels: 69.4 us -> 63.7 us
    pallas_call x1, Pallas kernels: 6.51 us -> 1.67 us  [per_device(): pl.pallas_call(hand_over, out_shape=tuple((shape(a.shape, a.dtype) for a...]
    pallas_call x1, Pallas kernels: 62.9 us -> 62 us  [per_device(): pl.pallas_call(functools.partial(kernel, R, F), out_shape=out_shapes, in_...]
where the time goes in v4:
time: 65.1 us; the launch traced here: 65 us
  Pallas kernels  63.7 us (98%)
  between operations  1.3 us (2%)
    pallas_call x1, Pallas kernels, per_device(): pl.pallas_call(functools.partial(kernel, R, F), out_shape=out_shapes, in_...  62 us
    pallas_call x1, Pallas kernels, per_device(): pl.pallas_call(hand_over, out_shape=tuple((shape(a.shape, a.dtype) for a...  1.67 us

profile of v4, /device:TPU:1, one launch (start us, length us, event | category | flops | bytes accessed | tf_op | source)
XLA Modules:
  0.0 65.0 jit_solution(4658191624987204917)
XLA Ops:
  1.3 62.0 %mixer.1 = (bf16[1,16,160]{2,1,0:T(8,128)(2,1)}, f32[1,5,64,128]{3,2,1,0:T(8,128)}, bf16[1,3,320]{2,1,0:T(4,128)(2,1)}, bf16[1,3,256]{2,1,0:T(4,128)(2,1)}) custom-call(bf16[1,16,2560]{2,1,0:T(8,128)(2,1)} %refs_0_.1, bf16[80,320]{1,0:T(8,128)(2,1)} %refs_1_.1, bf16[80,320]{1,0:T(8,128)(2,1)} %refs_2_.1, bf16[80,256]{1,0:T(8,128)(2,1)} %refs_3_.1, ...), custom_call_target="tpu_custom_call" | custom-call | tf_op jit(solution)/shard_map/mixer/pallas_call | solution.py:772
  63.3 1.7 %hand_over.1 = (bf16[1,16,160]{2,1,0:T(8,128)(2,1)}, f32[1,5,64,128]{3,2,1,0:T(8,128)}, bf16[1,3,320]{2,1,0:T(4,128)(2,1)}, bf16[1,3,256]{2,1,0:T(4,128)(2,1)}) custom-call(bf16[1,16,160]{2,1,0:T(8,128)(2,1)} %get-tuple-element.8.refs_0_, f32[1,5,64,128]{3,2,1,0:T(8,128)} %get-tuple-element.9.refs_1_, bf16[1,3,320]{2,1,0:T(4,128)(2,1)} %get-tuple-element.10.refs_2_, ...), custom_call_target="tpu_custom_call" | custom-call | tf_op jit(solution)/shard_map/hand_over/pallas_call | solution.py:784

commit v5 on v4

--- a/solution.py
+++ b/solution.py
@@ -64,6 +64,22 @@
 
 def silu(v):
     return v * jax.nn.sigmoid(v)
+
+
+def far_first(k, n):
+    return n // 2 + jnp.where(lax.rem(k, 2) == 1, -lax.div(k + 1, 2), lax.div(k, 2))
+
+
+def sum_blocks(ref):
+    n = ref.shape[0]
+    group = min(8, n)
+    total = None
+    for i in range(0, n, group):
+        part = ref[i].astype(f32)
+        for j in range(i + 1, i + group):
+            part = part + ref[j].astype(f32)
+        total = part if total is None else total + part
+    return total
 
 
 def pieces3(v):
@@ -151,8 +167,6 @@
     cc_all,
     state_buf,
     least_buf,
-    q_buf,
-    cum_buf,
     w5,
     pa_send,
     pa_recv,
@@ -184,27 +198,38 @@
     my = lax.div(me, X)
     mx = lax.rem(me, X)
     is_self = lax.div(mf, per_row) == my
+    source = lax.div(mf, per_row) * X + mx
+    Z = F // 2
+
+    def req_peer(i):
+        yy = lax.rem(my + far_first(lax.div(i, X), Y), Y)
+        return yy * X + lax.rem(mx + far_first(lax.rem(i, X), X), X)
+
+    def y_peer(i):
+        return lax.rem(my + far_first(i, Y), Y)
+
+    def f_peer(i):
+        zz = lax.rem(lax.div(mf, 2) + far_first(lax.div(i, 2), Z), Z)
+        return zz * 2 + lax.rem(mf + 1 + i, 2)
+
 
     load(*FIRST)
     barrier = pltpu.get_barrier_semaphore()
 
-    @pl.loop(1, R)
+    @pl.loop(0, R - 1)
     def _(i):
         pl.semaphore_signal(
-            barrier, inc=1, device_id={"req": lax.rem(me + i, R)}, device_id_type=MESH
+            barrier, inc=1, device_id={"req": req_peer(i)}, device_id_type=MESH
         )
 
-    @pl.loop(1, F)
-    def _(i):
-        pl.semaphore_signal(
-            barrier, inc=1, device_id={"fsdp": lax.rem(mf + i, F)}, device_id_type=MESH
-        )
-
-    source = lax.div(mf, per_row) * X + mx
+    @pl.loop(0, F - 1)
+    def _(i):
+        pl.semaphore_signal(barrier, inc=1, device_id={"fsdp": f_peer(i)}, device_id_type=MESH)
+
 
     @pl.loop(0, F)
     def _(i):
-        g = lax.rem(mf + i, F)
+        g = f_peer(i)
 
         @pl.when(jnp.logical_or(g != mf, source != me))
         def _():
@@ -255,9 +280,9 @@
     w_bytes = wxz.at[pl.ds(0, (X - 1) * ks), :]
     o_bytes = w_ext.at[pl.ds(0, (X - 1) * ocols), :]
 
-    @pl.loop(1, R)
-    def _(i):
-        put(w_own, w_all.at[:, own_lanes], 0, {"req": lax.rem(me + i, R)})
+    @pl.loop(0, R - 1)
+    def _(i):
+        put(w_own, w_all.at[:, own_lanes], 0, {"req": req_peer(i)})
 
     load(*OTHERS)
 
@@ -309,9 +334,9 @@
         ).astype(bf16)
     d_all[y_rows, :] = a_buf[pl.ds(0, T), pl.ds(pl.multiple_of(my * X * LN, X * LN), X * LN)]
 
-    @pl.loop(1, Y)
-    def _(i):
-        yy = lax.rem(my + i, Y)
+    @pl.loop(0, Y - 1)
+    def _(i):
+        yy = y_peer(i)
         put(
             a_buf.at[pl.ds(0, T), pl.ds(pl.multiple_of(yy * X * LN, X * LN), X * LN)],
             d_all.at[y_rows, :],
@@ -339,23 +364,22 @@
     arrive("cbb", "cbw", "cxb", "cxw", "gain", "ssm", "page_x", "page_b", "page_decay")
 
     wait_bytes(w_all.at[:, pl.ds(0, (R - 1) * LN)], recv_sem.at[0])
-    proj = nt(a_buf[pl.ds(0, 3 * T), :], w_all[...])
-    z_own[:, pl.ds(0, 3 * T)] = nt((iota((T, T), 0) == iota((T, T), 1)).astype(bf16), proj.astype(bf16)).astype(bf16)
+    z_own[:, pl.ds(0, 3 * T)] = nt(w_all[...], a_buf[...]).astype(bf16)
     z_rows = pl.ds(pl.multiple_of(mf * T, T), T)
     z_all[z_rows, :] = z_own[...]
 
-    @pl.loop(1, F)
-    def _(i):
-        put(z_own, z_all.at[z_rows, :], 2, {"fsdp": lax.rem(mf + i, F)})
+    @pl.loop(0, F - 1)
+    def _(i):
+        put(z_own, z_all.at[z_rows, :], 2, {"fsdp": f_peer(i)})
 
     wait_bytes(d_all.at[pl.ds(0, (Y - 1) * T), :], recv_sem.at[1])
     wait_bytes(w_bytes, recv_sem.at[8])
     xz_send[...] = jnp.dot(d_all[...], wxz[...], preferred_element_type=f32).astype(bf16)
     xz_recv[my] = xz_send[y_rows, :]
 
-    @pl.loop(1, Y)
-    def _(i):
-        yy = lax.rem(my + i, Y)
+    @pl.loop(0, Y - 1)
+    def _(i):
+        yy = y_peer(i)
         put(
             xz_send.at[pl.ds(pl.multiple_of(yy * T, T), T), :],
             xz_recv.at[my],
@@ -365,10 +389,11 @@
 
     er = iota((T, LN), 0)
     el = iota((T, LN), 1)
+    proj = nt(a_buf[pl.ds(T, 2 * T), :], w_all[...])
     first = ((er == el) & (el < heads)).astype(f32)
     second = ((er == el + heads) & (el < heads)).astype(f32)
-    dt_raw = jnp.dot(proj[T : 2 * T], first, precision=EXACT, preferred_element_type=f32) + jnp.dot(
-        proj[2 * T : 3 * T], second, precision=EXACT, preferred_element_type=f32
+    dt_raw = jnp.dot(proj[:T], first, precision=EXACT, preferred_element_type=f32) + jnp.dot(
+        proj[T:], second, precision=EXACT, preferred_element_type=f32
     )
     v = dt_raw + head_buf[pl.ds(0, 1), :]
     dtime = jnp.maximum(v, 0.0) + jnp.log1p(jnp.exp(-jnp.abs(v)))
@@ -401,9 +426,9 @@
     cc_own[pl.ds(T, 8), :] = packed.astype(bf16)
     cc_all[me] = cc_own[...]
 
-    @pl.loop(1, R)
-    def _(i):
-        put(cc_own, cc_all.at[me], 3, {"req": lax.rem(me + i, R)})
+    @pl.loop(0, R - 1)
+    def _(i):
+        put(cc_own, cc_all.at[me], 3, {"req": req_peer(i)})
 
     eye_h = iota((heads, LN), 0) == iota((heads, LN), 1)
 
@@ -429,21 +454,15 @@
         guarded = jnp.maximum(req, 0)
         live_of.append((req >= 0) & (slot_page_ref[s] < page_count_ref[guarded]))
         rows_of.append(owner_row_ref[guarded])
-    by_sub = jnp.zeros((slots * T, 1), jnp.int32)
     by_lane = jnp.zeros((1, slots * T), jnp.int32)
     live_sub = jnp.zeros((slots * T, 1), jnp.int32)
     for s in range(slots):
         in_sub = lax.div(iota((slots * T, 1), 0), T) == s
         in_lane = lax.div(iota((1, slots * T), 1), T) == s
-        by_sub = jnp.where(in_sub, rows_of[s], by_sub)
         live_sub = jnp.where(in_sub, live_of[s].astype(jnp.int32), live_sub)
         by_lane = jnp.where(
             in_lane, jnp.where(live_of[s], rows_of[s], -(1 << 20)), by_lane
         )
-    wide_lane = iota((slots * T, R * CROWS), 1)
-    at = lax.rem(iota((slots * T, 1), 0), T)
-    gather_c = (wide_lane == CROWS * by_sub + at).astype(bf16)
-    gather_cum = (wide_lane == CROWS * by_sub + T + lax.div(at, 8)).astype(bf16)
     at = lax.rem(iota((1, slots * T), 1), T)
     tall_sub = iota((R * 8, slots * T), 0)
     scatter_low = ((tall_sub == 8 * by_lane + at) & (at < 8)).astype(bf16)
@@ -458,16 +477,18 @@
         return out
 
     wait_bytes(cc_all.at[pl.ds(0, R - 1)], recv_sem.at[3])
-    cc = cc_all[...].reshape(R * CROWS, LN)
-    q_buf[...] = jnp.dot(gather_c, cc, preferred_element_type=f32)[:, :ns].astype(bf16)
-    cum3 = jnp.dot(gather_cum, cc, preferred_element_type=f32)
-    at = lax.rem(iota((slots * T, LN), 0), T)
-    el = iota((slots * T, LN), 1)
-    cum3 = jnp.where(lax.div(el, T) == lax.rem(at, 8), cum3, 0.0)
-    for step in (64, 32, 16):
-        cum3 = cum3 + pltpu.roll(cum3, step, 1)
-    cum = cum3 + pltpu.roll(cum3, LN - 5, 1) + pltpu.roll(cum3, LN - 10, 1)
-    cum_buf[...] = cum
+    group = lax.div(lane, T) == lax.rem(row, 8)
+    queries = []
+    fades = []
+    for s in range(slots):
+        block = cc_all[rows_of[s]]
+        queries.append(block[:T, :ns])
+        folded = block[T:].astype(f32)
+        folded = jnp.where(group, jnp.where(row < 8, folded[0:1], folded[1:2]), 0.0)
+        for step in (64, 32, 16):
+            folded = folded + pltpu.roll(folded, step, 1)
+        cum = folded + pltpu.roll(folded, LN - 5, 1) + pltpu.roll(folded, LN - 10, 1)
+        fades.append(jnp.exp(cum - least_buf[s]))
 
     cut = 2 * HD
     for first_head, send, recv, phase in ((0, pa_send, pa_recv, 5), (2, pb_send, pb_recv, 10)):
@@ -476,12 +497,11 @@
         lane_head = lax.div(iota((T, lanes), 1), HD) + first_head
         chosen = []
         for s in range(slots):
-            rows = pl.ds(s * T, T)
-            factor = jnp.exp(cum_buf[rows, :] - least_buf[s])
+            factor = fades[s]
             spread = jnp.zeros((T, lanes), f32)
             for h in range(first_head, first_head + lanes // HD):
                 spread = jnp.where(lane_head == h, factor[:, h : h + 1], spread)
-            chosen.append(nt(q_buf[rows, :], state_buf[s, part, :]) * spread)
+            chosen.append(nt(queries[s], state_buf[s, part, :]) * spread)
         kept = jnp.where(live_sub != 0, jnp.concatenate(chosen, axis=0), 0.0).astype(bf16)
         low = jnp.dot(scatter_low, kept, preferred_element_type=f32)
         high = jnp.dot(scatter_high, kept, preferred_element_type=f32)
@@ -489,15 +509,13 @@
         send[:, :, pl.ds(lanes, lanes)] = high.astype(bf16).reshape(R, 8, lanes)
         recv[me] = send[me]
 
-        @pl.loop(1, R)
+        @pl.loop(0, R - 1)
         def _(i, send=send, recv=recv, phase=phase):
-            r = lax.rem(me + i, R)
+            r = req_peer(i)
             put(send.at[r], recv.at[me], phase, {"req": r})
 
     wait_bytes(xz_recv.at[pl.ds(0, Y - 1)], recv_sem.at[4])
-    xz = lax.fori_loop(
-        1, Y, lambda i, total: total + xz_recv[i].astype(f32), xz_recv[0].astype(f32)
-    )
+    xz = sum_blocks(xz_recv)
     x_raw = xz[:, :inner].astype(bf16).astype(f32)
     z_raw = xz[:, inner:].astype(bf16).astype(f32)
     s_x[pl.ds(T, T), :] = x_raw
@@ -557,9 +575,7 @@
     parts = []
     for recv, phase in ((pa_recv, 5), (pb_recv, 10)):
         wait_bytes(recv.at[pl.ds(0, R - 1)], recv_sem.at[phase])
-        part = lax.fori_loop(
-            1, R, lambda i, total, recv=recv: total + recv[i].astype(f32), recv[0].astype(f32)
-        )
+        part = sum_blocks(recv)
         lanes = part.shape[1] // 2
         parts.append(jnp.concatenate([part[:, :lanes], part[:, lanes:]], axis=0))
     page_sum = jnp.concatenate(parts, axis=1)
@@ -573,9 +589,9 @@
     ).astype(bf16)
     g_all[y_rows, :] = g_own[...]
 
-    @pl.loop(1, Y)
-    def _(i):
-        put(g_own, g_all.at[y_rows, :], 6, {"req": lax.rem(my + i, Y) * X + mx})
+    @pl.loop(0, Y - 1)
+    def _(i):
+        put(g_own, g_all.at[y_rows, :], 6, {"req": y_peer(i) * X + mx})
 
     wait_bytes(o_bytes, recv_sem.at[9])
     wait_bytes(g_all.at[pl.ds(0, (Y - 1) * T), :], recv_sem.at[6])
@@ -593,9 +609,9 @@
         def _():
             put(f_send.at[y_rows, lanes], f_recv.at[mf], 7, {"fsdp": target})
 
-        @pl.loop(1, Y)
+        @pl.loop(0, Y - 1)
         def _(i):
-            yy = lax.rem(my + i, Y)
+            yy = y_peer(i)
             put(
                 f_send.at[pl.ds(pl.multiple_of(yy * T, T), T), lanes],
                 f_recv.at[mf],
@@ -611,9 +627,7 @@
     def _():
         wait_bytes(f_recv, recv_sem.at[7])
 
-    out = lax.fori_loop(
-        1, F, lambda i, total: total + f_recv[i].astype(f32), f_recv[0].astype(f32)
-    )
+    out = sum_blocks(f_recv)
     wide = 2 * ocols
     total_squares = (
         out[:, wide : wide + 1] + out[:, wide + 1 : wide + 2] + out[:, wide + 2 : wide + 3]
@@ -748,8 +762,6 @@
         pltpu.VMEM((R, CROWS, LN), bf16),
         pltpu.VMEM((slots, inner, ns), bf16),
         pltpu.VMEM((slots, 1, LN), f32),
-        pltpu.VMEM((slots * T, ns), bf16),
-        pltpu.VMEM((slots * T, LN), f32),
         pltpu.VMEM((heads * T, page), bf16),
         pltpu.VMEM((R, 8, 4 * HD), bf16),
         pltpu.VMEM((R, 8, 4 * HD), bf16),

time: 65.1 us -> 62.2 us (0.955)
  Pallas kernels: 63.7 us -> 60.7 us
    pallas_call x1, Pallas kernels: 62 us -> 59.1 us  [per_device(): pl.pallas_call(functools.partial(kernel, R, F), out_shape=out_shapes, in_...]
where the time goes in v5:
time: 62.2 us; the launch traced here: 62 us
  Pallas kernels  60.7 us (98%)
  between operations  1.3 us (2%)
    pallas_call x1, Pallas kernels, per_device(): pl.pallas_call(functools.partial(kernel, R, F), out_shape=out_shapes, in_...  59.1 us
    pallas_call x1, Pallas kernels, per_device(): pl.pallas_call(hand_over, out_shape=tuple((shape(a.shape, a.dtype) for a...  1.67 us

profile of v5, /device:TPU:1, one launch (start us, length us, event | category | flops | bytes accessed | tf_op | source)
XLA Modules:
  0.0 62.0 jit_solution(15110494933855003932)
XLA Ops:
  1.3 59.1 %mixer.1 = (bf16[1,16,160]{2,1,0:T(8,128)(2,1)}, f32[1,5,64,128]{3,2,1,0:T(8,128)}, bf16[1,3,320]{2,1,0:T(4,128)(2,1)}, bf16[1,3,256]{2,1,0:T(4,128)(2,1)}) custom-call(bf16[1,16,2560]{2,1,0:T(8,128)(2,1)} %refs_0_.1, bf16[80,320]{1,0:T(8,128)(2,1)} %refs_1_.1, bf16[80,320]{1,0:T(8,128)(2,1)} %refs_2_.1, bf16[80,256]{1,0:T(8,128)(2,1)} %refs_3_.1, ...), custom_call_target="tpu_custom_call" | custom-call | tf_op jit(solution)/shard_map/mixer/pallas_call | solution.py:784
  60.4 1.7 %hand_over.1 = (bf16[1,16,160]{2,1,0:T(8,128)(2,1)}, f32[1,5,64,128]{3,2,1,0:T(8,128)}, bf16[1,3,320]{2,1,0:T(4,128)(2,1)}, bf16[1,3,256]{2,1,0:T(4,128)(2,1)}) custom-call(bf16[1,16,160]{2,1,0:T(8,128)(2,1)} %get-tuple-element.8.refs_0_, f32[1,5,64,128]{3,2,1,0:T(8,128)} %get-tuple-element.9.refs_1_, bf16[1,3,320]{2,1,0:T(4,128)(2,1)} %get-tuple-element.10.refs_2_, ...), custom_call_target="tpu_custom_call" | custom-call | tf_op jit(solution)/shard_map/hand_over/pallas_call | solution.py:796

commit v6 on v5

--- a/solution.py
+++ b/solution.py
@@ -9,7 +9,7 @@
 
 MESH = pl.DeviceIdType.MESH
 T = 16
-CROWS = 24
+CROWS = 18
 X = 4
 KC = 4
 HD = 64
@@ -227,16 +227,6 @@
         pl.semaphore_signal(barrier, inc=1, device_id={"fsdp": f_peer(i)}, device_id_type=MESH)
 
 
-    @pl.loop(0, F)
-    def _(i):
-        g = f_peer(i)
-
-        @pl.when(jnp.logical_or(g != mf, source != me))
-        def _():
-            pl.semaphore_signal(
-                barrier, inc=1, device_id={"req": source, "fsdp": g}, device_id_type=MESH
-            )
-
     load(*SECOND)
     arrive("bcw", "dtw")
     wpad = jnp.concatenate([bcw_ref[...], jnp.zeros((LN - ks, 2 * ns), bf16)], axis=0)
@@ -260,7 +250,7 @@
     own_rows = pl.ds(pl.multiple_of(me * T, T), T)
     y_rows = pl.ds(pl.multiple_of(my * T, T), T)
     pl.semaphore_wait(
-        barrier, (R - 1) + (F - 1) + Y * per_row - is_self.astype(jnp.int32)
+        barrier, (R - 1) + (F - 1)
     )
 
     def put(src, dst, phase, device):
@@ -306,11 +296,6 @@
         top = pl.ds(2 * LN * i + 2 * ocols, rest)
         w_ext[top, pl.ds(0, inner)] = jnp.zeros((rest, inner), bf16)
         w_ext[top, pl.ds(inner, tail)] = ((er == el) & (el < 3)).astype(bf16)
-
-    @pl.loop(1, X)
-    def _(i):
-        r = my * X + lax.rem(mx + i, X)
-        put(wxz.at[own_block, :], wxz.at[own_block, :], 8, {"req": r})
 
     arrive("drafts")
     z_own[...] = jnp.zeros(z_own.shape, bf16)
@@ -334,21 +319,6 @@
         ).astype(bf16)
     d_all[y_rows, :] = a_buf[pl.ds(0, T), pl.ds(pl.multiple_of(my * X * LN, X * LN), X * LN)]
 
-    @pl.loop(0, Y - 1)
-    def _(i):
-        yy = y_peer(i)
-        put(
-            a_buf.at[pl.ds(0, T), pl.ds(pl.multiple_of(yy * X * LN, X * LN), X * LN)],
-            d_all.at[y_rows, :],
-            1,
-            {"req": yy * X + mx},
-        )
-
-    @pl.loop(1, X)
-    def _(i):
-        r = my * X + lax.rem(mx + i, X)
-        put(w_ext.at[own_outs, :], w_ext.at[own_outs, :], 9, {"req": r})
-
     arrive("dt_bias", "decay", "cbs", "cxs", "sink_b", "sink_x")
     head_buf[...] = jnp.zeros(head_buf.shape, f32)
     head_buf[pl.ds(0, 1), pl.ds(0, heads)] = dt_bias_ref[...].reshape(1, heads)
@@ -372,18 +342,18 @@
     def _(i):
         put(z_own, z_all.at[z_rows, :], 2, {"fsdp": f_peer(i)})
 
-    wait_bytes(d_all.at[pl.ds(0, (Y - 1) * T), :], recv_sem.at[1])
-    wait_bytes(w_bytes, recv_sem.at[8])
-    xz_send[...] = jnp.dot(d_all[...], wxz[...], preferred_element_type=f32).astype(bf16)
-    xz_recv[my] = xz_send[y_rows, :]
+    @pl.loop(1, X)
+    def _(i):
+        r = my * X + lax.rem(mx + i, X)
+        put(wxz.at[own_block, :], wxz.at[own_block, :], 8, {"req": r})
 
     @pl.loop(0, Y - 1)
     def _(i):
         yy = y_peer(i)
         put(
-            xz_send.at[pl.ds(pl.multiple_of(yy * T, T), T), :],
-            xz_recv.at[my],
-            4,
+            a_buf.at[pl.ds(0, T), pl.ds(pl.multiple_of(yy * X * LN, X * LN), X * LN)],
+            d_all.at[y_rows, :],
+            1,
             {"req": yy * X + mx},
         )
 
@@ -423,7 +393,7 @@
     if ns < LN:
         cc_own[...] = jnp.zeros(cc_own.shape, bf16)
     cc_own[pl.ds(0, T), pl.ds(0, ns)] = c_mat
-    cc_own[pl.ds(T, 8), :] = packed.astype(bf16)
+    cc_own[pl.ds(T, CROWS - T), :] = packed[: CROWS - T].astype(bf16)
     cc_all[me] = cc_own[...]
 
     @pl.loop(0, R - 1)
@@ -445,6 +415,26 @@
                 faded.astype(bf16), page_b_ref[s], preferred_element_type=f32
             ).astype(bf16)
 
+
+    wait_bytes(d_all.at[pl.ds(0, (Y - 1) * T), :], recv_sem.at[1])
+    wait_bytes(w_bytes, recv_sem.at[8])
+    xz_send[...] = jnp.dot(d_all[...], wxz[...], preferred_element_type=f32).astype(bf16)
+    xz_recv[my] = xz_send[y_rows, :]
+
+    @pl.loop(0, Y - 1)
+    def _(i):
+        yy = y_peer(i)
+        put(
+            xz_send.at[pl.ds(pl.multiple_of(yy * T, T), T), :],
+            xz_recv.at[my],
+            4,
+            {"req": yy * X + mx},
+        )
+
+    @pl.loop(1, X)
+    def _(i):
+        r = my * X + lax.rem(mx + i, X)
+        put(w_ext.at[own_outs, :], w_ext.at[own_outs, :], 9, {"req": r})
 
     arrive("slot_req", "slot_page", "page_count", "owner_row", "accepted")
     rows_of = []

time: 62.2 us -> 60.7 us (0.976)
  Pallas kernels: 60.7 us -> 59.2 us
    pallas_call x1, Pallas kernels: 59.1 us -> 57.5 us  [per_device(): pl.pallas_call(functools.partial(kernel, R, F), out_shape=out_shapes, in_...]
where the time goes in v6:
time: 60.7 us; the launch traced here: 60.5 us
  Pallas kernels  59.2 us (98%)
  between operations  1.3 us (2%)
    pallas_call x1, Pallas kernels, per_device(): pl.pallas_call(functools.partial(kernel, R, F), out_shape=out_shapes, in_...  57.5 us
    pallas_call x1, Pallas kernels, per_device(): pl.pallas_call(hand_over, out_shape=tuple((shape(a.shape, a.dtype) for a...  1.67 us

profile of v6, /device:TPU:1, one launch (start us, length us, event | category | flops | bytes accessed | tf_op | source)
XLA Modules:
  0.0 60.5 jit_solution(6376535755683358715)
XLA Ops:
  1.3 57.5 %mixer.1 = (bf16[1,16,160]{2,1,0:T(8,128)(2,1)}, f32[1,5,64,128]{3,2,1,0:T(8,128)}, bf16[1,3,320]{2,1,0:T(4,128)(2,1)}, bf16[1,3,256]{2,1,0:T(4,128)(2,1)}) custom-call(bf16[1,16,2560]{2,1,0:T(8,128)(2,1)} %refs_0_.1, bf16[80,320]{1,0:T(8,128)(2,1)} %refs_1_.1, bf16[80,320]{1,0:T(8,128)(2,1)} %refs_2_.1, bf16[80,256]{1,0:T(8,128)(2,1)} %refs_3_.1, ...), custom_call_target="tpu_custom_call" | custom-call | tf_op jit(solution)/shard_map/mixer/pallas_call | solution.py:774
  58.8 1.7 %hand_over.1 = (bf16[1,16,160]{2,1,0:T(8,128)(2,1)}, f32[1,5,64,128]{3,2,1,0:T(8,128)}, bf16[1,3,320]{2,1,0:T(4,128)(2,1)}, bf16[1,3,256]{2,1,0:T(4,128)(2,1)}) custom-call(bf16[1,16,160]{2,1,0:T(8,128)(2,1)} %get-tuple-element.8.refs_0_, f32[1,5,64,128]{3,2,1,0:T(8,128)} %get-tuple-element.9.refs_1_, bf16[1,3,320]{2,1,0:T(4,128)(2,1)} %get-tuple-element.10.refs_2_, ...), custom_call_target="tpu_custom_call" | custom-call | tf_op jit(solution)/shard_map/hand_over/pallas_call | solution.py:786

commit v7 on v6

--- a/solution.py
+++ b/solution.py
@@ -201,9 +201,12 @@
     source = lax.div(mf, per_row) * X + mx
     Z = F // 2
 
-    def req_peer(i):
-        yy = lax.rem(my + far_first(lax.div(i, X), Y), Y)
-        return yy * X + lax.rem(mx + far_first(lax.rem(i, X), X), X)
+    def ring(n):
+        return [n // 2 + (-(k + 1) // 2 if k % 2 else k // 2) for k in range(n)]
+
+    y_ring = [lax.rem(my + k, Y) * X for k in ring(Y)]
+    x_ring = [lax.rem(mx + k, X) for k in ring(X)]
+    req_peers = [a + b for a in y_ring for b in x_ring][: R - 1]
 
     def y_peer(i):
         return lax.rem(my + far_first(i, Y), Y)
@@ -216,11 +219,8 @@
     load(*FIRST)
     barrier = pltpu.get_barrier_semaphore()
 
-    @pl.loop(0, R - 1)
-    def _(i):
-        pl.semaphore_signal(
-            barrier, inc=1, device_id={"req": req_peer(i)}, device_id_type=MESH
-        )
+    for r in req_peers:
+        pl.semaphore_signal(barrier, inc=1, device_id={"req": r}, device_id_type=MESH)
 
     @pl.loop(0, F - 1)
     def _(i):
@@ -270,9 +270,8 @@
     w_bytes = wxz.at[pl.ds(0, (X - 1) * ks), :]
     o_bytes = w_ext.at[pl.ds(0, (X - 1) * ocols), :]
 
-    @pl.loop(0, R - 1)
-    def _(i):
-        put(w_own, w_all.at[:, own_lanes], 0, {"req": req_peer(i)})
+    for r in req_peers:
+        put(w_own, w_all.at[:, own_lanes], 0, {"req": r})
 
     load(*OTHERS)
 
@@ -396,9 +395,8 @@
     cc_own[pl.ds(T, CROWS - T), :] = packed[: CROWS - T].astype(bf16)
     cc_all[me] = cc_own[...]
 
-    @pl.loop(0, R - 1)
-    def _(i):
-        put(cc_own, cc_all.at[me], 3, {"req": req_peer(i)})
+    for r in req_peers:
+        put(cc_own, cc_all.at[me], 3, {"req": r})
 
     eye_h = iota((heads, LN), 0) == iota((heads, LN), 1)
 
@@ -499,9 +497,7 @@
         send[:, :, pl.ds(lanes, lanes)] = high.astype(bf16).reshape(R, 8, lanes)
         recv[me] = send[me]
 
-        @pl.loop(0, R - 1)
-        def _(i, send=send, recv=recv, phase=phase):
-            r = req_peer(i)
+        for r in req_peers:
             put(send.at[r], recv.at[me], phase, {"req": r})
 
     wait_bytes(xz_recv.at[pl.ds(0, Y - 1)], recv_sem.at[4])

time: 60.7 us -> 60 us (0.988)
  Pallas kernels: 59.2 us -> 58.5 us
    pallas_call x1, Pallas kernels: 57.5 us -> 56.8 us  [per_device(): pl.pallas_call(functools.partial(kernel, R, F), out_shape=out_shapes, in_...]
where the time goes in v7:
time: 60 us; the launch traced here: 59.8 us
  Pallas kernels  58.5 us (98%)
  between operations  1.3 us (2%)
    pallas_call x1, Pallas kernels, per_device(): pl.pallas_call(functools.partial(kernel, R, F), out_shape=out_shapes, in_...  56.8 us
    pallas_call x1, Pallas kernels, per_device(): pl.pallas_call(hand_over, out_shape=tuple((shape(a.shape, a.dtype) for a...  1.67 us

profile of v7, /device:TPU:1, one launch (start us, length us, event | category | flops | bytes accessed | tf_op | source)
XLA Modules:
  0.0 59.8 jit_solution(11585919909293471738)
XLA Ops:
  1.3 56.8 %mixer.1 = (bf16[1,16,160]{2,1,0:T(8,128)(2,1)}, f32[1,5,64,128]{3,2,1,0:T(8,128)}, bf16[1,3,320]{2,1,0:T(4,128)(2,1)}, bf16[1,3,256]{2,1,0:T(4,128)(2,1)}) custom-call(bf16[1,16,2560]{2,1,0:T(8,128)(2,1)} %refs_0_.1, bf16[80,320]{1,0:T(8,128)(2,1)} %refs_1_.1, bf16[80,320]{1,0:T(8,128)(2,1)} %refs_2_.1, bf16[80,256]{1,0:T(8,128)(2,1)} %refs_3_.1, ...), custom_call_target="tpu_custom_call" | custom-call | tf_op jit(solution)/shard_map/mixer/pallas_call | solution.py:770
  58.1 1.7 %hand_over.1 = (bf16[1,16,160]{2,1,0:T(8,128)(2,1)}, f32[1,5,64,128]{3,2,1,0:T(8,128)}, bf16[1,3,320]{2,1,0:T(4,128)(2,1)}, bf16[1,3,256]{2,1,0:T(4,128)(2,1)}) custom-call(bf16[1,16,160]{2,1,0:T(8,128)(2,1)} %get-tuple-element.8.refs_0_, f32[1,5,64,128]{3,2,1,0:T(8,128)} %get-tuple-element.9.refs_1_, bf16[1,3,320]{2,1,0:T(4,128)(2,1)} %get-tuple-element.10.refs_2_, ...), custom_call_target="tpu_custom_call" | custom-call | tf_op jit(solution)/shard_map/hand_over/pallas_call | solution.py:782
